TPU v7x, 32 devices: a whole 2x2x4 slice. The times are simulated.
32 devices in a mesh: groups: 2 (over y), shot: 4 (over z), depth: 2 (over x), freq: 2 (over core).
Axes of the slice: x: 2, y: 2, z: 4, core: 2. Of those that a mesh axis runs over, the one named last changes fastest.
Arguments:
- source: float32 [8, 6, 2, 256, 256], P(('groups', 'shot'), 'freq'), parts along dimension 0, may hold values from -6 to 6
- receiver: float32 [8, 6, 2, 256, 256], P(('groups', 'shot'), 'freq'), parts along dimension 0, may hold values from -6 to 6
- slowness: float32 [8, 4, 256, 256], P(('groups', 'shot'), 'depth'), parts along dimension 0, may hold values from 0.6 to 1.4
- omegas: float32 [8, 6], P(('groups', 'shot'), 'freq'), parts along dimension 0, may hold values from 0.5 to 2.5
- shot_start: int32 [8], P(('groups', 'shot')), parts along dimension 0, may hold values from 0 to 256, as said below
Outputs:
- image: float32 [1024, 4, 256], P(('groups', 'shot'), 'depth', 'freq'), parts along dimension 0
There are 2 independent parts, one for each index of `groups`. A program takes and returns all parts, laid end to end along the dimension named above; each array names one. Nothing has to cross between parts.
Inputs may be any that keep to these rules, and one draw needn't show every extreme that they name: `shot_start`: any shot group's aperture may begin at any column of the survey. Shot group 4 // 2 begins at column 0 and shot group 0 at 256.
All inputs are finite; a program needn't handle non-finite values.
Results may differ from a plain program's by a relative error of at most 0.03.
Values may be sent and summed in bfloat16 or wider, within the bound.
No kernel may reach another device: no remote copies, remote signals or barrier semaphores. Data moves between devices by JAX's collectives and lax.ppermute only.
A program may use at most 64 MiB of HBM per device.

v0:
```python
import jax
import jax.numpy as jnp
from jax import lax
from jax.sharding import PartitionSpec as P

TILE = 128


def from_behind(array, axis, by):
    peers = lax.axis_size(axis)
    pairs = [(i, i + by) for i in range(peers) if 0 <= i + by < peers]
    return lax.ppermute(array, axis, pairs)


def tables(points):
    positions = jnp.arange(points, dtype=jnp.int32)
    product = positions[:, None] * positions[None, :] % points
    angles = 2.0 * jnp.pi / points * product.astype(jnp.float32)
    cosine_table = jnp.cos(angles).astype(jnp.bfloat16)
    sine_table = jnp.sin(angles).astype(jnp.bfloat16)
    forward = jnp.concatenate(
        [
            jnp.concatenate([cosine_table, -sine_table], axis=1),
            jnp.concatenate([sine_table, cosine_table], axis=1),
        ],
        axis=0,
    )
    inverse = jnp.concatenate(
        [
            jnp.concatenate([cosine_table, sine_table], axis=1),
            jnp.concatenate([-sine_table, cosine_table], axis=1),
        ],
        axis=0,
    )
    return (forward, inverse)


def lateral_grids(points):
    positions = jnp.arange(points, dtype=jnp.int32)
    wrapped = (positions + points // 2) % points - points // 2
    wavenumber = 2.0 * jnp.pi / points * wrapped.astype(jnp.float32)
    edge_width = points // 16
    distance_in = jnp.minimum(positions, points - 1 - positions) + 1
    edge_taper = jnp.minimum(distance_in.astype(jnp.float32) / edge_width, 1.0)
    return (wavenumber, edge_taper)


def flip_parts(field_in):
    leading = field_in.shape[:-2]
    row_count = field_in.shape[-2]
    col_count = field_in.shape[-1] // 2
    pieces = field_in.reshape(leading + (row_count, 2, col_count))
    moved = jnp.swapaxes(pieces, -3, -1)
    return moved.reshape(leading + (col_count, 2 * row_count))


def extrapolate(
    wave_state, slow_level, angular, field_signs, forward, inverse, wavenumber, edge_taper
):
    batch_size, points, width = wave_state.shape
    inv_points = 1.0 / points
    half_done = jnp.dot(
        wave_state.reshape(batch_size * points, width), forward, preferred_element_type=jnp.float32
    )
    half_done = flip_parts(half_done.astype(jnp.bfloat16).reshape(batch_size, points, width))
    spectrum = jnp.dot(
        half_done.reshape(batch_size * points, width), forward, preferred_element_type=jnp.float32
    ).reshape(batch_size, points, width)
    mean_slow = jnp.mean(slow_level)
    radius_sq = jnp.square(angular * mean_slow)
    square = jnp.square(wavenumber)[:, None] + jnp.square(wavenumber)[None, :]
    vertical = radius_sq[:, None, None] - square[None]
    real_kz = jnp.sqrt(jnp.maximum(vertical, 0.0))
    damping = jnp.exp(-jnp.sqrt(jnp.maximum(-vertical, 0.0)))
    phase_turn = field_signs[:, None, None] * real_kz
    phase_real = damping * jnp.cos(phase_turn)
    phase_imag = damping * jnp.sin(phase_turn)
    spec_real = spectrum[..., :points]
    spec_imag = spectrum[..., points:]
    shifted = jnp.concatenate(
        [
            spec_real * phase_real - spec_imag * phase_imag,
            spec_real * phase_imag + spec_imag * phase_real,
        ],
        axis=-1,
    ).astype(jnp.bfloat16)
    half_back = (
        jnp.dot(
            shifted.reshape(batch_size * points, width), inverse, preferred_element_type=jnp.float32
        )
        * inv_points
    )
    half_back = flip_parts(half_back.astype(jnp.bfloat16).reshape(batch_size, points, width))
    field_out = (
        jnp.dot(
            half_back.reshape(batch_size * points, width),
            inverse,
            preferred_element_type=jnp.float32,
        ).reshape(batch_size, points, width)
        * inv_points
    )
    correction = (field_signs * angular)[:, None, None] * (slow_level - mean_slow)[None]
    window = edge_taper[:, None] * edge_taper[None, :]
    corr_real = jnp.cos(correction) * window[None]
    corr_imag = jnp.sin(correction) * window[None]
    field_real = field_out[..., :points]
    field_imag = field_out[..., points:]
    return (
        field_real * corr_real - field_imag * corr_imag,
        field_real * corr_imag + field_imag * corr_real,
    )


def local(source, receiver, slowness, omegas, shot_start):
    points = source.shape[-1]
    fronts = source.shape[1]
    levels = slowness.shape[1]
    segments = lax.axis_size("depth")
    segment_index = lax.axis_index("depth")
    forward, inverse = tables(points)
    wavenumber, edge_taper = lateral_grids(points)
    field_signs = jnp.array([-1.0, 1.0], jnp.float32)

    def surface(chosen):
        src_front = lax.dynamic_index_in_dim(source[0], chosen, 0, keepdims=False)
        rcv_front = lax.dynamic_index_in_dim(receiver[0], chosen, 0, keepdims=False)
        paired = jnp.stack([src_front, rcv_front])
        return jnp.concatenate([paired[:, 0], paired[:, 1]], axis=-1).astype(jnp.bfloat16)

    def extrapolate_front(operands):
        wave_state, rate_now = operands
        angular = jnp.stack([rate_now, rate_now])
        level_terms = []
        for level_index in range(levels):
            real_part, imag_part = extrapolate(
                wave_state,
                slowness[0, level_index],
                angular,
                field_signs,
                forward,
                inverse,
                wavenumber,
                edge_taper,
            )
            level_terms.append(real_part[0] * real_part[1] + imag_part[0] * imag_part[1])
            wave_state = jnp.concatenate([real_part, imag_part], axis=-1).astype(jnp.bfloat16)
        return (wave_state, jnp.stack(level_terms, axis=1))

    def stay_still(operands):
        wave_state, rate_now = operands
        return (jnp.zeros_like(wave_state), jnp.zeros((points, levels, points), jnp.float32))

    def one_turn(turn_index, carry):
        incoming, image_sum = carry
        front_index = turn_index - segment_index
        active = jnp.logical_and(front_index >= 0, front_index < fronts)
        chosen = jnp.clip(front_index, 0, fronts - 1)
        begin_field = jnp.where(segment_index == 0, surface(chosen), incoming)
        rate_now = lax.dynamic_index_in_dim(omegas[0], chosen, 0, keepdims=False)
        wave_state, level_image = lax.cond(
            active, extrapolate_front, stay_still, (begin_field, rate_now)
        )
        incoming = from_behind(wave_state, "depth", 1)
        return (incoming, image_sum + level_image)

    initial = (
        jnp.zeros((2, points, 2 * points), jnp.bfloat16),
        jnp.zeros((points, levels, points), jnp.float32),
    )
    final_carry = lax.fori_loop(0, segments + fronts - 1, one_turn, initial)
    local_image = lax.psum_scatter(
        final_carry[1].astype(jnp.bfloat16), "freq", scatter_dimension=2, tiled=True
    ).astype(jnp.float32)
    aperture_start = shot_start[0]
    owners = lax.axis_size("shot")
    survey_cols = owners * TILE
    padding = jnp.zeros((survey_cols,) + local_image.shape[1:], jnp.float32)
    padded = jnp.concatenate([padding, local_image, padding], axis=0)
    offset = jnp.clip(
        jnp.zeros((), jnp.int32) - aperture_start + survey_cols, 0, points + survey_cols
    )
    placed = lax.dynamic_slice_in_dim(padded, offset, survey_cols, 0)
    blocks = placed.reshape((owners, TILE) + local_image.shape[1:])
    received = lax.all_to_all(
        blocks.astype(jnp.bfloat16), "shot", split_axis=0, concat_axis=0, tiled=True
    ).astype(blocks.dtype)
    collected = jnp.sum(received, axis=0)
    return collected


def solution(mesh):
    return jax.shard_map(
        local,
        mesh=mesh,
        in_specs=(
            P(("groups", "shot"), "freq", None, None, None),
            P(("groups", "shot"), "freq", None, None, None),
            P(("groups", "shot"), "depth", None, None),
            P(("groups", "shot"), "freq"),
            P(("groups", "shot")),
        ),
        out_specs=P(("groups", "shot"), "depth", "freq"),
        check_vma=False,
    )
```

profile of v0, /device:TPU:0, one launch (start us, length us, event | category | flops | bytes accessed | tf_op | source)
XLA Modules:
  0.0 212.3 jit_solution(7978232508442241251)
XLA Ops:
  6.5 1.1 sine_convert_fusion
  8.7 2.4 %convert.56 = bf16[1,3,2,256,256]{4,3,2,1,0:T(8,128)(2,1)} convert(f32[1,3,2,256,256]{4,3,2,1,0:T(8,128)} %param.10) | non-fusion elementwise | flops 393216 | bytes 2359296
  13.1 164.7 %while.19 = (s32[]{:T(128)}, bf16[2,256,512]{2,1,0:T(8,128)(2,1)S(1)}, f32[256,2,256]{2,0,1:T(8,128)}, s32[]{:T(128)}, bf16[1,3,2,256,256]{4,3,2,1,0:T(8,128)(2,...) while((s32[]{:T(128)}, ...), condition=%wide.region_5.6_spmd.clone.clone.clone, body=%wide.region_0.5_spmd.sunk.clone.clone.clone.sunk | while | flops 2163611136 | bytes 54534728 | solution.py:170
  13.1 1.1 dynamic-slice_bitcast_fusion.3
  14.3 25.3 %conditional.6 = (bf16[2,256,512]{2,1,0:T(8,128)(2,1)}, f32[256,2,256]{2,0,1:T(8,128)S(1)}) conditional(s32[]{:T(128)} %convert_element_type.155, () %tuple.108, (pred[]{:T(512)}, bf16[2,256,512]{2,1,0:T(8,128)(2,1)S(1)}, bf16[2,256,512]{2,1,0:T(8,128)(2,1)S(1)}, bf16[512,512]{1,0:T(8,128)(2,1)S(1)}, f32[1,3]{1,0:T(1,128)S(1)}, ...), branch_computations={%region_1.1_spmd, %region_2.4_spmd.clone} | conditional | flops 2162033664 | bytes 46668028 | solution.py:160
  18.1 1.0 copy.37
  20.1 2.7 %subtract_convert_fusion.1 = (bf16[2,256,256]{2,1,0:T(8,128)(2,1)S(1)}, bf16[2,256,256]{2,1,0:T(8,128)(2,1)S(1)}) fusion(f32[2,256,512]{2,1,0:T(8,128)S(1)} %fusion.55, f32[2]{0:T(128)S(1)} %copy-done.3, f32[256,256]{1,0:T(8,128)S(1)} %broadcast_add_fusion, f32[2]{0:T(128)S(1)} %get-tuple-element.564), kind=kLoop, calls=%fused_computation.74 | loop fusion | flops 2097152 | bytes 1835024 | tf_op jit(solution)/shard_map/convert.13
  23.4 1.0 copy.38
  26.6 2.1 %fusion.86 = (bf16[2,256,256]{2,1,0:T(8,128)(2,1)S(1)}, f32[2,256,256]{2,1,0:T(8,128)S(1)}, bf16[2,256,256]{2,1,0:T(8,128)(2,1)S(1)}, f32[2,256,256]{2,1,0:T(8,128)S(1)}) fusion(f32[2,256,512]{2,1,0:T(8,128)S(1)} %convolution_multiply_fusion.2, f32[256,256]{1,0:T(8,128)S(1)} %broadcast_multiply_fusion, f32[256,256]{1,0:T(8,128)S(1)} %get-tuple-element.560, ...), kind=kLoop, calls=%fused_computation.143 | loop fusion | flops 1441792 | bytes 3145736 | tf_op jit(solution)/shard_map/convert.9
  29.4 1.0 copy.39
  31.2 2.7 %subtract_convert_fusion = (bf16[2,256,256]{2,1,0:T(8,128)(2,1)S(1)}, bf16[2,256,256]{2,1,0:T(8,128)(2,1)S(1)}) fusion(f32[2,256,512]{2,1,0:T(8,128)S(1)} %fusion.53, f32[2]{0:T(128)S(1)} %get-tuple-element.563, f32[2]{0:T(128)S(1)} %copy-done.3, f32[256,256]{1,0:T(8,128)S(1)} %broadcast_add_fusion), kind=kLoop, calls=%fused_computation.72 | loop fusion | flops 2097152 | bytes 1835024 | tf_op jit(solution)/shard_map/convert.5
  34.5 1.0 copy.40
  36.5 2.1 %fusion.82 = (bf16[2,256,256]{2,1,0:T(8,128)(2,1)S(1)}, f32[2,256,256]{2,1,0:T(8,128)S(1)}, bf16[2,256,256]{2,1,0:T(8,128)(2,1)S(1)}, f32[2,256,256]{2,1,0:T(8,128)S(1)}) fusion(f32[2,256,512]{2,1,0:T(8,128)S(1)} %convolution_multiply_fusion, f32[256,256]{1,0:T(8,128)S(1)} %broadcast_multiply_fusion, f32[256,256]{1,0:T(8,128)S(1)} %copy-done.1, f32[2]{0:T(128)S(1)} %fusion.64), kind=kLoop, calls=%fused_computation.141 | loop fusion | flops 1441792 | bytes 3145736 | tf_op jit(solution)/shard_map/convert
  39.6 1.3 collective-permute-start
  41.8 11.5 %collective-permute-done = bf16[2,256,512]{2,1,0:T(8,128)(2,1)S(1)} collective-permute-done((bf16[2,256,512]{2,1,0:T(8,128)(2,1)}, bf16[2,256,512]{2,1,0:T(8,128)(2,1)S(1)}, u32[]{:S(2)}, u32[]{:S(2)}) %collective-permute-start) | collective-permute-done | bytes 524320 | tf_op jit(solution)/shard_map/while/body/eval_jaxpr/ppermute | solution.py:12
  53.3 1.1 dynamic-slice_bitcast_fusion.3
  54.5 25.3 %conditional.6 = (bf16[2,256,512]{2,1,0:T(8,128)(2,1)}, f32[256,2,256]{2,0,1:T(8,128)S(1)}) conditional(s32[]{:T(128)} %convert_element_type.155, () %tuple.108, (pred[]{:T(512)}, bf16[2,256,512]{2,1,0:T(8,128)(2,1)S(1)}, bf16[2,256,512]{2,1,0:T(8,128)(2,1)S(1)}, bf16[512,512]{1,0:T(8,128)(2,1)S(1)}, f32[1,3]{1,0:T(1,128)S(1)}, ...), branch_computations={%region_1.1_spmd, %region_2.4_spmd.clone} | conditional | flops 2162033664 | bytes 46668028 | solution.py:160
  58.3 1.0 copy.37
  60.3 2.7 %subtract_convert_fusion.1 = (bf16[2,256,256]{2,1,0:T(8,128)(2,1)S(1)}, bf16[2,256,256]{2,1,0:T(8,128)(2,1)S(1)}) fusion(f32[2,256,512]{2,1,0:T(8,128)S(1)} %fusion.55, f32[2]{0:T(128)S(1)} %copy-done.3, f32[256,256]{1,0:T(8,128)S(1)} %broadcast_add_fusion, f32[2]{0:T(128)S(1)} %get-tuple-element.564), kind=kLoop, calls=%fused_computation.74 | loop fusion | flops 2097152 | bytes 1835024 | tf_op jit(solution)/shard_map/convert.13
  63.6 1.0 copy.38
  66.8 2.1 %fusion.86 = (bf16[2,256,256]{2,1,0:T(8,128)(2,1)S(1)}, f32[2,256,256]{2,1,0:T(8,128)S(1)}, bf16[2,256,256]{2,1,0:T(8,128)(2,1)S(1)}, f32[2,256,256]{2,1,0:T(8,128)S(1)}) fusion(f32[2,256,512]{2,1,0:T(8,128)S(1)} %convolution_multiply_fusion.2, f32[256,256]{1,0:T(8,128)S(1)} %broadcast_multiply_fusion, f32[256,256]{1,0:T(8,128)S(1)} %get-tuple-element.560, ...), kind=kLoop, calls=%fused_computation.143 | loop fusion | flops 1441792 | bytes 3145736 | tf_op jit(solution)/shard_map/convert.9
  69.7 1.0 copy.39
  71.4 2.7 %subtract_convert_fusion = (bf16[2,256,256]{2,1,0:T(8,128)(2,1)S(1)}, bf16[2,256,256]{2,1,0:T(8,128)(2,1)S(1)}) fusion(f32[2,256,512]{2,1,0:T(8,128)S(1)} %fusion.53, f32[2]{0:T(128)S(1)} %get-tuple-element.563, f32[2]{0:T(128)S(1)} %copy-done.3, f32[256,256]{1,0:T(8,128)S(1)} %broadcast_add_fusion), kind=kLoop, calls=%fused_computation.72 | loop fusion | flops 2097152 | bytes 1835024 | tf_op jit(solution)/shard_map/convert.5
  74.7 1.0 copy.40
  76.7 2.1 %fusion.82 = (bf16[2,256,256]{2,1,0:T(8,128)(2,1)S(1)}, f32[2,256,256]{2,1,0:T(8,128)S(1)}, bf16[2,256,256]{2,1,0:T(8,128)(2,1)S(1)}, f32[2,256,256]{2,1,0:T(8,128)S(1)}) fusion(f32[2,256,512]{2,1,0:T(8,128)S(1)} %convolution_multiply_fusion, f32[256,256]{1,0:T(8,128)S(1)} %broadcast_multiply_fusion, f32[256,256]{1,0:T(8,128)S(1)} %copy-done.1, f32[2]{0:T(128)S(1)} %fusion.64), kind=kLoop, calls=%fused_computation.141 | loop fusion | flops 1441792 | bytes 3145736 | tf_op jit(solution)/shard_map/convert
  79.8 4.3 %collective-permute-start = (bf16[2,256,512]{2,1,0:T(8,128)(2,1)}, bf16[2,256,512]{2,1,0:T(8,128)(2,1)S(1)}, u32[]{:S(2)}, u32[]{:S(2)}) collective-permute-start(bf16[2,256,512]{2,1,0:T(8,128)(2,1)} %get-tuple-element.656), channel_id=1, source_target_pairs={{0,2},{1,3},{4,6},{5,7},{8,10},{9,11},{12,14},{13,15},{16,18},{17,... | collective-permute-start | bytes 1572872 | tf_op jit(solution)/shard_map/while/body/eval_jaxpr/ppermute | solution.py:12
  84.1 1.9 select_add_fusion.2
  86.0 9.6 %collective-permute-done = bf16[2,256,512]{2,1,0:T(8,128)(2,1)S(1)} collective-permute-done((bf16[2,256,512]{2,1,0:T(8,128)(2,1)}, bf16[2,256,512]{2,1,0:T(8,128)(2,1)S(1)}, u32[]{:S(2)}, u32[]{:S(2)}) %collective-permute-start) | collective-permute-done | bytes 524320 | tf_op jit(solution)/shard_map/while/body/eval_jaxpr/ppermute | solution.py:12
  95.7 1.1 dynamic-slice_bitcast_fusion.3
  96.9 25.3 %conditional.6 = (bf16[2,256,512]{2,1,0:T(8,128)(2,1)}, f32[256,2,256]{2,0,1:T(8,128)S(1)}) conditional(s32[]{:T(128)} %convert_element_type.155, () %tuple.108, (pred[]{:T(512)}, bf16[2,256,512]{2,1,0:T(8,128)(2,1)S(1)}, bf16[2,256,512]{2,1,0:T(8,128)(2,1)S(1)}, bf16[512,512]{1,0:T(8,128)(2,1)S(1)}, f32[1,3]{1,0:T(1,128)S(1)}, ...), branch_computations={%region_1.1_spmd, %region_2.4_spmd.clone} | conditional | flops 2162033664 | bytes 46668028 | solution.py:160
  100.7 1.0 copy.37
  102.6 2.7 %subtract_convert_fusion.1 = (bf16[2,256,256]{2,1,0:T(8,128)(2,1)S(1)}, bf16[2,256,256]{2,1,0:T(8,128)(2,1)S(1)}) fusion(f32[2,256,512]{2,1,0:T(8,128)S(1)} %fusion.55, f32[2]{0:T(128)S(1)} %copy-done.3, f32[256,256]{1,0:T(8,128)S(1)} %broadcast_add_fusion, f32[2]{0:T(128)S(1)} %get-tuple-element.564), kind=kLoop, calls=%fused_computation.74 | loop fusion | flops 2097152 | bytes 1835024 | tf_op jit(solution)/shard_map/convert.13
  105.9 1.0 copy.38
  109.2 2.1 %fusion.86 = (bf16[2,256,256]{2,1,0:T(8,128)(2,1)S(1)}, f32[2,256,256]{2,1,0:T(8,128)S(1)}, bf16[2,256,256]{2,1,0:T(8,128)(2,1)S(1)}, f32[2,256,256]{2,1,0:T(8,128)S(1)}) fusion(f32[2,256,512]{2,1,0:T(8,128)S(1)} %convolution_multiply_fusion.2, f32[256,256]{1,0:T(8,128)S(1)} %broadcast_multiply_fusion, f32[256,256]{1,0:T(8,128)S(1)} %get-tuple-element.560, ...), kind=kLoop, calls=%fused_computation.143 | loop fusion | flops 1441792 | bytes 3145736 | tf_op jit(solution)/shard_map/convert.9
  112.0 1.0 copy.39
  113.8 2.7 %subtract_convert_fusion = (bf16[2,256,256]{2,1,0:T(8,128)(2,1)S(1)}, bf16[2,256,256]{2,1,0:T(8,128)(2,1)S(1)}) fusion(f32[2,256,512]{2,1,0:T(8,128)S(1)} %fusion.53, f32[2]{0:T(128)S(1)} %get-tuple-element.563, f32[2]{0:T(128)S(1)} %copy-done.3, f32[256,256]{1,0:T(8,128)S(1)} %broadcast_add_fusion), kind=kLoop, calls=%fused_computation.72 | loop fusion | flops 2097152 | bytes 1835024 | tf_op jit(solution)/shard_map/convert.5
  117.1 1.0 copy.40
  119.1 2.1 %fusion.82 = (bf16[2,256,256]{2,1,0:T(8,128)(2,1)S(1)}, f32[2,256,256]{2,1,0:T(8,128)S(1)}, bf16[2,256,256]{2,1,0:T(8,128)(2,1)S(1)}, f32[2,256,256]{2,1,0:T(8,128)S(1)}) fusion(f32[2,256,512]{2,1,0:T(8,128)S(1)} %convolution_multiply_fusion, f32[256,256]{1,0:T(8,128)S(1)} %broadcast_multiply_fusion, f32[256,256]{1,0:T(8,128)S(1)} %copy-done.1, f32[2]{0:T(128)S(1)} %fusion.64), kind=kLoop, calls=%fused_computation.141 | loop fusion | flops 1441792 | bytes 3145736 | tf_op jit(solution)/shard_map/convert
  122.2 4.3 %collective-permute-start = (bf16[2,256,512]{2,1,0:T(8,128)(2,1)}, bf16[2,256,512]{2,1,0:T(8,128)(2,1)S(1)}, u32[]{:S(2)}, u32[]{:S(2)}) collective-permute-start(bf16[2,256,512]{2,1,0:T(8,128)(2,1)} %get-tuple-element.656), channel_id=1, source_target_pairs={{0,2},{1,3},{4,6},{5,7},{8,10},{9,11},{12,14},{13,15},{16,18},{17,... | collective-permute-start | bytes 1572872 | tf_op jit(solution)/shard_map/while/body/eval_jaxpr/ppermute | solution.py:12
  126.5 1.9 select_add_fusion.2
  128.4 8.8 %collective-permute-done = bf16[2,256,512]{2,1,0:T(8,128)(2,1)S(1)} collective-permute-done((bf16[2,256,512]{2,1,0:T(8,128)(2,1)}, bf16[2,256,512]{2,1,0:T(8,128)(2,1)S(1)}, u32[]{:S(2)}, u32[]{:S(2)}) %collective-permute-start) | collective-permute-done | bytes 524320 | tf_op jit(solution)/shard_map/while/body/eval_jaxpr/ppermute | solution.py:12
  137.2 1.1 dynamic-slice_bitcast_fusion.3
  139.3 28.7 %collective-permute-start = (bf16[2,256,512]{2,1,0:T(8,128)(2,1)}, bf16[2,256,512]{2,1,0:T(8,128)(2,1)S(1)}, u32[]{:S(2)}, u32[]{:S(2)}) collective-permute-start(bf16[2,256,512]{2,1,0:T(8,128)(2,1)} %get-tuple-element.656), channel_id=1, source_target_pairs={{0,2},{1,3},{4,6},{5,7},{8,10},{9,11},{12,14},{13,15},{16,18},{17,... | collective-permute-start | bytes 1572872 | tf_op jit(solution)/shard_map/while/body/eval_jaxpr/ppermute | solution.py:12
  168.0 1.9 select_add_fusion.2
  169.9 7.9 %collective-permute-done = bf16[2,256,512]{2,1,0:T(8,128)(2,1)S(1)} collective-permute-done((bf16[2,256,512]{2,1,0:T(8,128)(2,1)}, bf16[2,256,512]{2,1,0:T(8,128)(2,1)S(1)}, u32[]{:S(2)}, u32[]{:S(2)}) %collective-permute-start) | collective-permute-done | bytes 524320 | tf_op jit(solution)/shard_map/while/body/eval_jaxpr/ppermute | solution.py:12
  177.8 1.1 convert_element_type.110
  180.4 8.2 %reduce-scatter.4.cloned.1.call-done = bf16[128,512]{1,0:T(8,128)(2,1)} async-done(((bf16[256,512]{1,0:T(8,128)(2,1)}), bf16[128,512]{1,0:T(8,128)(2,1)}) %reduce-scatter.4.cloned.1.call-update) | async-done | bytes 131088
  190.6 14.0 %all_to_all.5 = bf16[4,128,2,128]{3,1,2,0:T(8,128)(2,1)S(1)} all-to-all(bf16[4,128,2,128]{3,1,2,0:T(8,128)(2,1)S(1)} %copy.33), channel_id=1, replica_groups=mesh['groups'=2,'shot'=4,'depth'=2,'freq'=2] {'shot'}, dimensions={0} | all-to-all | bytes 524288 | tf_op jit(solution)/shard_map/all_to_all | solution.py:184
  (141 shorter events, 39.9 us)
Async XLA Ops:
  6.5 4.5 %copy-start.2 = (f32[1,3,2,256,256]{4,3,2,1,0:T(8,128)S(1)}, f32[1,3,2,256,256]{4,3,2,1,0:T(8,128)}, u32[]{:S(2)}) copy-start(f32[1,3,2,256,256]{4,3,2,1,0:T(8,128)} %param.11) | copy-start | bytes 4718596
  6.5 182.1 %reduce-scatter.4.cloned.1.call-start = ((), (), s32[]{:S(2)}) async-start(), calls=%async_computation.2 | async-start | bytes 393216
  12.0 1.0 copy-start
  12.0 1.0 copy-start.4
  19.1 0.9 copy-start.3
  35.5 1.0 copy-start.1
  39.6 13.7 %collective-permute-start = (bf16[2,256,512]{2,1,0:T(8,128)(2,1)}, bf16[2,256,512]{2,1,0:T(8,128)(2,1)S(1)}, u32[]{:S(2)}, u32[]{:S(2)}) collective-permute-start(bf16[2,256,512]{2,1,0:T(8,128)(2,1)} %get-tuple-element.656), channel_id=1, source_target_pairs={{0,2},{1,3},{4,6},{5,7},{8,10},{9,11},{12,14},{13,15},{16,18},{17,... | collective-permute-start | bytes 1572872 | tf_op jit(solution)/shard_map/while/body/eval_jaxpr/ppermute | solution.py:12
  59.4 0.9 copy-start.3
  75.7 1.0 copy-start.1
  79.8 15.8 %collective-permute-start = (bf16[2,256,512]{2,1,0:T(8,128)(2,1)}, bf16[2,256,512]{2,1,0:T(8,128)(2,1)S(1)}, u32[]{:S(2)}, u32[]{:S(2)}) collective-permute-start(bf16[2,256,512]{2,1,0:T(8,128)(2,1)} %get-tuple-element.656), channel_id=1, source_target_pairs={{0,2},{1,3},{4,6},{5,7},{8,10},{9,11},{12,14},{13,15},{16,18},{17,... | collective-permute-start | bytes 1572872 | tf_op jit(solution)/shard_map/while/body/eval_jaxpr/ppermute | solution.py:12
  101.7 0.9 copy-start.3
  118.1 1.0 copy-start.1
  122.2 15.0 %collective-permute-start = (bf16[2,256,512]{2,1,0:T(8,128)(2,1)}, bf16[2,256,512]{2,1,0:T(8,128)(2,1)S(1)}, u32[]{:S(2)}, u32[]{:S(2)}) collective-permute-start(bf16[2,256,512]{2,1,0:T(8,128)(2,1)} %get-tuple-element.656), channel_id=1, source_target_pairs={{0,2},{1,3},{4,6},{5,7},{8,10},{9,11},{12,14},{13,15},{16,18},{17,... | collective-permute-start | bytes 1572872 | tf_op jit(solution)/shard_map/while/body/eval_jaxpr/ppermute | solution.py:12
  139.3 38.5 %collective-permute-start = (bf16[2,256,512]{2,1,0:T(8,128)(2,1)}, bf16[2,256,512]{2,1,0:T(8,128)(2,1)S(1)}, u32[]{:S(2)}, u32[]{:S(2)}) collective-permute-start(bf16[2,256,512]{2,1,0:T(8,128)(2,1)} %get-tuple-element.656), channel_id=1, source_target_pairs={{0,2},{1,3},{4,6},{5,7},{8,10},{9,11},{12,14},{13,15},{16,18},{17,... | collective-permute-start | bytes 1572872 | tf_op jit(solution)/shard_map/while/body/eval_jaxpr/ppermute | solution.py:12
Sparse Core Ops, SparseCore 0:
  179.9 8.7 reduce-scatter.3
where the time goes:
time: 213 us; the launch traced here: 212 us
  other arithmetic  55.5 us (26%)
  waiting for transfers between devices  46 us (22%)
  starting transfers between devices  38.6 us (18%)
  local copies, waits for them, and re-layouts  28.8 us (14%)
  between operations  14.1 us (7%)
  blocking collectives  14 us (7%)
  matrix products  10.4 us (5%)
  loops' own time  4.77 us (2%)
    ppermute x4, starting transfers between devices, from_behind(): return lax.ppermute(array, axis, pairs)  38.6 us
    ppermute x4, waiting for transfers between devices, from_behind(): return lax.ppermute(array, axis, pairs)  37.7 us
    another operation x16, other arithmetic  29.4 us
    all_to_all x1, blocking collectives, local(): lax.all_to_all(blocks.astype(jnp.bfloat16), 'shot', split_axis=0, concat_...  14 us
    transpose x12, local copies, waits for them, and re-layouts, flip_parts(): moved = jnp.swapaxes(pieces, -3, -1)  12 us
    unnamed x2, waiting for transfers between devices  8.24 us
    add x4, other arithmetic, one_turn(): return (incoming, image_sum + level_image)  6.64 us
    another operation x4, loops' own time, one_turn(): lax.cond(active, extrapolate_front, stay_still, (begin_field, rate_now))  4.55 us
  transfers between devices with their start and end apart: 5, of which 5 were waited for; matrix products, arithmetic and copies ran while one was open for 3% of the time, Pallas kernels for 0%

commit v1 on v0

v1 whole, which is shorter than its diff:
```python
import functools

import jax
import jax.numpy as jnp
import ml_dtypes
import numpy as np
from jax import lax
from jax.experimental import pallas as pl
from jax.experimental.pallas import tpu as pltpu
from jax.sharding import PartitionSpec as P_

TILE = 128

def _fit(f, hi, deg):
    k = np.arange(400)
    x = (np.cos(np.pi * (k + 0.5) / 400) + 1) / 2 * hi
    c = np.polynomial.chebyshev.Chebyshev.fit(x, f(x), deg, domain=[0, hi])
    return [float(v) for v in c.convert(kind=np.polynomial.Polynomial).coef]
def _cosr(a): return np.cos(np.sqrt(a))
def _sinr(a): return np.sinc(np.sqrt(a) / np.pi)
PC = _fit(_cosr, 12.5, 6); PS = _fit(_sinr, 12.5, 5)
CC = _fit(_cosr, 4.1, 5); CS = _fit(_sinr, 4.1, 4)

def horner(co, x):
    r = co[-1] * x + co[-2]
    for c in co[-3::-1]:
        r = r * x + c
    return r

def make_tables(n):
    h, g = n // 2, n // 4
    idx = np.arange(n)
    ang = 2 * np.pi / n * (np.outer(idx, idx) % n)
    C = np.cos(ang).astype(ml_dtypes.bfloat16).astype(np.float32)
    S = np.sin(ang).astype(ml_dtypes.bfloat16).astype(np.float32)
    i = np.arange(g)
    ev = np.concatenate([2 * i, np.where(i == 0, h, n - 2 * i)])
    od = np.concatenate([2 * i + 1, n - 2 * i - 1])
    out = []
    for k in (ev, od):
        c, s = C[:h][:, k], S[:h][:, k]
        F = np.block([[c, -s], [s, c]])
        L = np.block([[c.T, s.T], [-s.T, c.T]])
        out.append((F, L, F / 1.0, L))
    T = []
    for p in (0, 1):
        k = (ev, od)[p]
        c, s = C[:h][:, k], S[:h][:, k]
        T.append(np.stack([np.block([[c, -s], [s, c]]), np.block([[c.T, s.T], [-s.T, c.T]]),
                           np.block([[c, -s], [s, c]]) / n, np.block([[c.T, s.T], [-s.T, c.T]]) / n]))
    T = np.stack(T, axis=1).astype(ml_dtypes.bfloat16)
    w = ((idx + h) % n - h).astype(np.float32)
    kk = (np.float32(2 * np.pi) / np.float32(n) * w).astype(np.float32)
    k2 = (kk * kk).astype(np.float32)
    base = np.concatenate([k2[2 * i], k2[2 * i + 1]])
    rows = np.concatenate([base, k2[h:h + 1]])
    K2 = np.zeros((h + 8, h), np.float32)
    K2[:h + 1] = rows[:, None] + base[None, :]
    K2[h + 1] = k2[h] + k2[h]
    ed = np.minimum(np.minimum(idx, n - 1 - idx) + 1, n // 16).astype(np.float32) / np.float32(n // 16)
    win = (ed[:, None] * ed[None, :]).astype(np.float32)
    return T, K2, win

def level_prep(n, s, win, D):
    s0 = jnp.sum(s[...]) * (1.0 / (n * n))
    d = s[...] - s0
    D[0] = d * d
    D[1] = d * win[...]
    return s0

def propagator(n, w2, K2, P):
    h, g = n // 2, n // 4
    a = w2 - K2[...]
    pos = a >= 0.0
    r = jnp.sqrt(jnp.abs(a))
    vals = (jnp.where(pos, horner(PC, a), jnp.exp(-r)), jnp.where(pos, r * horner(PS, a), 0.0))
    lane = lax.broadcasted_iota(jnp.int32, (8, h), 1)
    low, mid = lane < g, lane == g
    row0 = lax.broadcasted_iota(jnp.int32, (8, n), 0) == 0
    for comp in (0, 1):
        v = vals[comp]
        col = jnp.broadcast_to(v[h:h + 1], (h, h)).T
        for t in range(h // 8 + 1):
            p = v[8 * t:8 * t + 8]
            q = pltpu.roll(p, g, 1)
            cc = col[8 * t:8 * t + 8] if t < h // 8 else jnp.broadcast_to(v[h + 1:h + 2, :], (8, h))
            e = jnp.where(mid, cc, jnp.where(low, p, q))
            o = jnp.where(low, q, p)
            if t < g // 8:
                P[comp, 8 * t:8 * t + 8, :h] = e
                P[comp, 8 * t:8 * t + 8, h:] = o
                if t == 0:
                    e0, o0 = e, o
            elif t < h // 8:
                P[comp, 8 * t + 8:8 * t + 16, :h] = e
                P[comp, 8 * t + 8:8 * t + 16, h:] = o
            else:
                P[comp, g:g + 8, :h] = jnp.where(row0[:, :h], e, e0)
                P[comp, g:g + 8, h:] = jnp.where(row0[:, :h], o, o0)

def p_rows(n, P, comp, par):
    h, g = n // 2, n // 4
    if par == 0:
        return jnp.concatenate([P[comp, 0:g], P[comp, g:g + 8], P[comp, 8:g]], axis=0)
    o = P[comp, g + 8:h + 8]
    return jnp.concatenate([o, o], axis=0)

def corr(n, om, win, D, c):
    o2 = om * om
    cc, cs, f = [], [], jnp.float32(1.0)
    for k in range(max(len(CC), len(CS))):
        if k < len(CC): cc.append(CC[k] * f)
        if k < len(CS): cs.append(CS[k] * f * om)
        f = f * o2
    x = D[0]
    c[0] = win[...] * horner(cc, x)
    c[1] = D[1] * horner(cs, x)

def front_math(n, om, s0, T, K2, win, st, part, P, c, D):
    h = n // 2
    f32, bf = jnp.float32, jnp.bfloat16
    dot = functools.partial(jnp.dot, preferred_element_type=f32)
    w2 = om * s0; w2 = w2 * w2
    FL = ((0, -1.0), (1, 1.0))
    add, sub = (lambda a, b: a + b), (lambda a, b: a - b)
    def stack2(X, Y, op):
        re = jnp.concatenate([op(X[:h, :h], X[h:, :h]), op(Y[:h, :h], Y[h:, :h])], axis=1)
        im = jnp.concatenate([op(X[:h, h:], X[h:, h:]), op(Y[:h, h:], Y[h:, h:])], axis=1)
        return jnp.concatenate([re, im], axis=0).astype(bf)
    R = []
    for f, sg in FL:
        Ve = dot(st[f, 0], T[0, 0]); Vo = dot(st[f, 1], T[0, 1])
        R.append((stack2(Ve, Vo, add), stack2(Ve, Vo, sub)))
    propagator(n, w2, K2, P)
    W2 = []
    for f, sg in FL:
        out = []
        for p in (0, 1):
            W = dot(T[1, p], R[f][p])
            wr, wi = W[:h], W[h:]
            pr, pi = p_rows(n, P, 0, p), p_rows(n, P, 1, p)
            if sg > 0:
                out.append(jnp.concatenate([wr * pr - wi * pi, wr * pi + wi * pr], axis=0).astype(bf))
            else:
                out.append(jnp.concatenate([wr * pr + wi * pi, wi * pr - wr * pi], axis=0).astype(bf))
        W2.append(out)
    corr(n, om, win, D, c)
    YY = []
    for f, sg in FL:
        E = dot(T[2, 0], W2[f][0]); O = dot(T[2, 1], W2[f][1])
        U, Dn = E + O, E - O
        out = []
        for p in (0, 1):
            sl = slice(p * h, (p + 1) * h)
            out.append(jnp.concatenate([jnp.concatenate([U[:h, sl], U[h:, sl]], axis=1),
                                        jnp.concatenate([Dn[:h, sl], Dn[h:, sl]], axis=1)], axis=0).astype(bf))
        YY.append(out)
    res = []
    for f, sg in FL:
        Q0, Q1 = dot(YY[f][0], T[3, 0]), dot(YY[f][1], T[3, 1])
        X, Z = Q0 + Q1, Q0 - Q1
        halves = []
        for hf, q in ((0, X), (1, Z)):
            qr, qi = q[:, :h], q[:, h:]
            cr, ci = c[0, :, hf * h:(hf + 1) * h], c[1, :, hf * h:(hf + 1) * h]
            if sg > 0:
                halves.append((qr * cr - qi * ci, qr * ci + qi * cr))
            else:
                halves.append((qr * cr + qi * ci, qi * cr - qr * ci))
        (r0, i0), (r1, i1) = halves
        st[f, 0] = jnp.concatenate([r0 + r1, i0 + i1], axis=1).astype(bf)
        st[f, 1] = jnp.concatenate([r0 - r1, i0 - i1], axis=1).astype(bf)
        res.append(halves)
    for hf in (0, 1):
        (ur, ui), (wr, wi) = res[0][hf], res[1][hf]
        sl = slice(hf * h, (hf + 1) * h)
        part[:, sl] = part[:, sl] + (ur * wr + ui * wi)

def prep(n, src, st_ab):
    h = n // 2
    bf = jnp.bfloat16
    st_ab[0] = jnp.concatenate([src[0, :, :h] + src[0, :, h:], src[1, :, :h] + src[1, :, h:]], axis=1).astype(bf)
    st_ab[1] = jnp.concatenate([src[0, :, :h] - src[0, :, h:], src[1, :, :h] - src[1, :, h:]], axis=1).astype(bf)


ANY = pl.BlockSpec(memory_space=pl.ANY)
VM = pl.BlockSpec(memory_space=pltpu.VMEM)
SM = pl.BlockSpec(memory_space=pltpu.SMEM)
F32, BF16 = jnp.float32, jnp.bfloat16


def params(mib):
    return pltpu.CompilerParams(vmem_limit_bytes=mib * 1024 * 1024)


def first_levels(dims, who, om, src, rcv, slow, T, K2, win, st_out, own_out, raw, st, P, c, D, sem_in, sem_out):
    n, slots, L = dims
    nf, f0, levels = who[0], who[1], who[2]

    def moves(j):
        fr = f0 + j
        return (
            pltpu.make_async_copy(src.at[fr], raw.at[j, 0], sem_in.at[j, 0]),
            pltpu.make_async_copy(rcv.at[fr], raw.at[j, 1], sem_in.at[j, 1]),
        )

    for j in range(slots):
        @pl.when(j < nf)
        def _(j=j):
            for m in moves(j):
                m.start()
    for j in range(slots):
        @pl.when(j < nf)
        def _(j=j):
            for f, m in enumerate(moves(j)):
                m.wait()
                prep(n, raw.at[j, f], st.at[j, f])

    def level(z, _):
        s0 = level_prep(n, slow.at[z], win, D)
        own_out[z] = jnp.zeros((n, n), F32)

        def front(j, _):
            front_math(n, om[f0 + j], s0, T, K2, win, st.at[j], own_out.at[z], P, c, D)
            return 0

        lax.fori_loop(0, nf, front, 0)
        return 0

    lax.fori_loop(0, levels, level, 0)
    out = pltpu.make_async_copy(st, st_out, sem_out)
    out.start()
    out.wait()


def other_levels(dims, who, om, st_in, slow, got, own_in, T, K2, win, keep_own, send_own, keep_oth, send_oth,
                 st, s_now, part, P, c, D, sem):
    n, L, depth, freq = dims
    nf, f0, lo, d, fq = who[0], who[1], who[2], who[3], who[4]
    w = n // freq
    move = pltpu.make_async_copy(st_in, st, sem)
    move.start()

    def split(ref, keep, sends):
        for a in range(freq):
            @pl.when(fq == a)
            def _():
                keep[...] = ref[:, a * w:(a + 1) * w]
                for r in range(1, freq):
                    b = (a + r) % freq
                    sends.at[r - 1][...] = ref[:, b * w:(b + 1) * w].astype(BF16)

    @pl.when(lo > 0)
    def _():
        for z in range(L):
            split(own_in.at[z], keep_own.at[z], send_own.at[:, z])

    move.wait()

    def level(z, _):
        owner = z // L
        zl = z - owner * L
        back = lax.rem(d - owner + depth, depth)

        @pl.when(back == 0)
        def _():
            s_now[...] = slow[zl]

        @pl.when(back > 0)
        def _():
            s_now[...] = got[jnp.maximum(back - 1, 0), zl].astype(F32) + 1.0

        s0 = level_prep(n, s_now, win, D)
        part[...] = jnp.zeros((n, n), F32)

        def front(j, _):
            front_math(n, om[f0 + j], s0, T, K2, win, st.at[j], part, P, c, D)
            return 0

        lax.fori_loop(0, nf, front, 0)

        @pl.when(back == 0)
        def _():
            split(part, keep_own.at[zl], send_own.at[:, zl])

        @pl.when(back > 0)
        def _():
            r = jnp.maximum(depth - back - 1, 0)
            split(part, keep_oth.at[r, zl], send_oth.at[:, r, zl])

        return 0

    lax.fori_loop(lo, depth * L, level, 0)


def place(dims, where, own, got, out, padded):
    n, L, shots, more = dims
    w = own.shape[-1]
    survey = shots * TILE
    me, begin = where[0], where[1]
    padded[:, :survey] = jnp.zeros((L, survey, w), F32)
    padded[:, survey + n:] = jnp.zeros((L, survey, w), F32)
    for z in range(L):
        total = own[z]
        for r in range(more):
            total = total + got[r, z].astype(F32)
        padded[z, survey:survey + n] = total
    for r in range(shots):
        owner = lax.rem(me + r, shots)
        offset = jnp.clip(owner * TILE - begin + survey, 0, n + survey)
        for z in range(L):
            out[r, z] = padded[z, pl.ds(offset, TILE), :].astype(BF16)


def gather(dims, *refs):
    L, shots = dims
    out = refs[-1]
    for z in range(L):
        total = refs[0][z].astype(F32)
        for r in range(1, shots):
            total = total + refs[r][z].astype(F32)
        out[:, z, :] = total


def shift(array, axis, by):
    size = lax.axis_size(axis)
    return lax.ppermute(array, axis, [(i, (i + by) % size) for i in range(size)])


def local(source, receiver, slowness, omegas, shot_start):
    n = source.shape[-1]
    h = n // 2
    fronts, L = source.shape[1], slowness.shape[1]
    depth, freq, shots = lax.axis_size("depth"), lax.axis_size("freq"), lax.axis_size("shot")
    d, fq, me = lax.axis_index("depth"), lax.axis_index("freq"), lax.axis_index("shot")
    T, K2, win = make_tables(n)
    slots = -(-fronts // depth)
    base, extra = fronts // depth, fronts % depth
    nf = base + jnp.where(d < extra, 1, 0)
    f0 = d * base + jnp.minimum(d, extra)
    w = n // freq
    S = jax.ShapeDtypeStruct
    V = pltpu.VMEM
    om, slow = omegas[0], slowness[0]

    sent = (slow - 1.0).astype(BF16)
    got = jnp.stack([shift(sent, "depth", r) for r in range(1, depth)])

    math_scratch = [V((2, h + 8, n), F32), V((2, n, n), F32), V((2, n, n), F32)]
    who = jnp.stack([nf, f0, jnp.where(d == 0, L, 0)]).astype(jnp.int32)
    state, own_a = pl.pallas_call(
        functools.partial(first_levels, (n, slots, L)),
        out_shape=(S((slots, 2, 2, n, n), BF16), S((L, n, n), F32)),
        in_specs=[SM, SM, ANY, ANY, VM, VM, VM, VM],
        out_specs=(ANY, VM),
        scratch_shapes=[V((slots, 2, 2, n, n), F32), V((slots, 2, 2, n, n), BF16)] + math_scratch
        + [pltpu.SemaphoreType.DMA((slots, 2)), pltpu.SemaphoreType.DMA],
        compiler_params=params(32),
        cost_estimate=pl.CostEstimate(flops=8 * 10**9, bytes_accessed=10**7, transcendentals=10**6),
        name="first_levels",
    )(who, om, source[0], receiver[0], slow, T, K2, win)

    who = jnp.stack([nf, f0, jnp.where(d == 0, L, 0), d, fq]).astype(jnp.int32)
    keep_own, send_own, keep_oth, send_oth = pl.pallas_call(
        functools.partial(other_levels, (n, L, depth, freq)),
        out_shape=(S((L, n, w), F32), S((freq - 1, L, n, w), BF16),
                   S((depth - 1, L, n, w), F32), S((freq - 1, depth - 1, L, n, w), BF16)),
        in_specs=[SM, SM, ANY, VM, VM, VM, VM, VM, VM],
        out_specs=(VM, VM, VM, VM),
        scratch_shapes=[V((slots, 2, 2, n, n), BF16), V((n, n), F32), V((n, n), F32)] + math_scratch
        + [pltpu.SemaphoreType.DMA],
        compiler_params=params(32),
        cost_estimate=pl.CostEstimate(flops=8 * 10**9, bytes_accessed=10**7, transcendentals=10**6),
        name="other_levels",
    )(who, om, state, slow, got, own_a, T, K2, win)

    own, oth = keep_own, keep_oth
    for r in range(1, freq):
        oth = oth + shift(send_oth[r - 1], "freq", r).astype(F32)
    for r in range(1, freq):
        own = own + shift(send_own[r - 1], "freq", r).astype(F32)
    oth = oth.astype(BF16)
    arrived = jnp.stack([shift(oth[r - 1], "depth", r) for r in range(1, depth)])

    where = jnp.stack([me, shot_start[0]]).astype(jnp.int32)
    blocks = pl.pallas_call(
        functools.partial(place, (n, L, shots, depth - 1)),
        out_shape=S((shots, L, TILE, w), BF16),
        in_specs=[SM, VM, VM],
        out_specs=VM,
        scratch_shapes=[V((L, 2 * shots * TILE + n, w), F32)],
        compiler_params=params(32),
        name="place",
    )(where, own, arrived)
    pieces = [blocks[0]] + [shift(blocks[r], "shot", r) for r in range(1, shots)]
    return pl.pallas_call(
        functools.partial(gather, (L, shots)),
        out_shape=S((TILE, L, w), F32),
        in_specs=[VM] * shots,
        out_specs=VM,
        compiler_params=params(16),
        name="gather",
    )(*pieces)


def solution(mesh):
    return jax.shard_map(
        local,
        mesh=mesh,
        in_specs=(
            P_(("groups", "shot"), "freq", None, None, None),
            P_(("groups", "shot"), "freq", None, None, None),
            P_(("groups", "shot"), "depth", None, None),
            P_(("groups", "shot"), "freq"),
            P_(("groups", "shot")),
        ),
        out_specs=P_(("groups", "shot"), "depth", "freq"),
        check_vma=False,
    )
```

time: 213 us -> 45.7 us (0.21)
  other arithmetic: 55.5 us -> 1.28 us
  waiting for transfers between devices: 46 us -> 10.7 us
  starting transfers between devices: 38.6 us -> 8.34 us
  local copies, waits for them, and re-layouts: 28.8 us -> 9.9 us
  Pallas kernels: 0 us -> 14.3 us
  blocking collectives: 14 us -> 0 us
  between operations: 14.1 us -> 0.78 us
  matrix products: 10.4 us -> 0 us
  loops' own time: 4.77 us -> 0 us
    ppermute x4 -> x7, starting transfers between devices: 38.6 us -> 8.34 us  [shift(): lax.ppermute(array, axis, [(i, (i + by) % size) for i in range(size)])]
    another operation x19 -> x2, other arithmetic: 29.5 us -> 0.15 us  [the longest x1 0.08 us: local(): who = jnp.stack([nf, f0, jnp.where(d == 0, L, 0)]).astype(jnp.int32)]
    ppermute x4 -> x7, waiting for transfers between devices: 37.7 us -> 10.7 us  [shift(): lax.ppermute(array, axis, [(i, (i + by) % size) for i in range(size)])]
    pallas_call x0 -> x4, Pallas kernels: none -> 14.3 us  [the longest x1 6.55 us: local(): pl.pallas_call(functools.partial(first_levels, (n, slots, L)), out_shape=...]
    all_to_all x1 -> x0, blocking collectives: 14 us -> none  [local(): lax.all_to_all(blocks.astype(jnp.bfloat16), 'shot', split_axis=0, concat_...]
    transpose x12 -> x0, local copies, waits for them, and re-layouts: 12 us -> none  [flip_parts(): moved = jnp.swapaxes(pieces, -3, -1)]
    dot_general x24 -> x0, matrix products: 10.4 us -> none  [the longest x6 2.62 us: extrapolate(): jnp.dot(shifted.reshape(batch_size * points, width), inverse, preferred_e...]
    unnamed x2 -> x0, waiting for transfers between devices: 8.24 us -> none
  transfers between devices with their start and end apart: 5 -> 7, of which waited for: 5 -> 6; matrix products, arithmetic and copies ran while one was open for 3% -> 1% of each run, Pallas kernels for 0% -> 14%
where the time goes in v1:
time: 45.7 us; the launch traced here: 45.3 us
  Pallas kernels  14.3 us (31%)
  waiting for transfers between devices  10.7 us (23%)
  local copies, waits for them, and re-layouts  9.9 us (22%)
  starting transfers between devices  8.34 us (18%)
  other arithmetic  1.28 us (3%)
  between operations  0.78 us (2%)
    ppermute x7, waiting for transfers between devices, shift(): lax.ppermute(array, axis, [(i, (i + by) % size) for i in range(size)])  10.7 us
    unnamed x28, local copies, waits for them, and re-layouts  9.8 us
    ppermute x7, starting transfers between devices, shift(): lax.ppermute(array, axis, [(i, (i + by) % size) for i in range(size)])  8.34 us
    pallas_call x1, Pallas kernels, local(): pl.pallas_call(functools.partial(first_levels, (n, slots, L)), out_shape=...  6.55 us
    pallas_call x1, Pallas kernels, local(): pl.pallas_call(functools.partial(other_levels, (n, L, depth, freq)), out_...  6.38 us
    convert_element_type x1, other arithmetic, local(): sent = (slow - 1.0).astype(BF16)  1.08 us
  transfers between devices with their start and end apart: 7, of which 6 were waited for; matrix products, arithmetic and copies ran while one was open for 1% of the time, Pallas kernels for 14%

profile of v1, /device:TPU:0, one launch (start us, length us, event | category | flops | bytes accessed | tf_op | source)
XLA Modules:
  0.0 45.3 jit_solution(18199453326137605151)
XLA Ops:
  0.0 1.1 %add_convert_fusion = bf16[2,256,256]{2,1,0:T(8,128)(2,1)S(1)} fusion(f32[1,2,256,256]{3,2,1,0:T(8,128)} %param.10), kind=kLoop, calls=%fused_computation | loop fusion | flops 262144 | bytes 786432 | tf_op jit(solution)/shard_map/convert_element_type | solution.py:346
  1.1 3.0 %collective-permute-start = (bf16[2,256,256]{2,1,0:T(8,128)(2,1)S(1)}, bf16[2,256,256]{2,1,0:T(8,128)(2,1)S(1)}, u32[]{:S(2)}, u32[]{:S(2)}) collective-permute-start(bf16[2,256,256]{2,1,0:T(8,128)(2,1)S(1)} %add_convert_fusion), channel_id=1, source_target_pairs={{0,2},{2,0},{1,3},{3,1},{4,6},{6,4},{5,7},{7,5},{8,10},{10,8},{9,1... | collective-permute-start | bytes 786440 | tf_op jit(solution)/shard_map/ppermute | solution.py:327
  4.1 0.1 pad_add_fusion.1.who
  4.2 0.0 copy-start
  4.2 1.0 %copy-done = f32[1,2,256,256]{3,2,1,0:T(8,128)S(1)} copy-done((f32[1,2,256,256]{3,2,1,0:T(8,128)S(1)}, f32[1,2,256,256]{3,2,1,0:T(8,128)}, u32[]{:S(2)}) %copy-start) | copy-done | bytes 524312
  5.2 0.0 copy-start.2
  5.2 1.4 %copy-done.2 = f32[1,3,2,256,256]{4,3,2,1,0:T(8,128)S(1)} copy-done((f32[1,3,2,256,256]{4,3,2,1,0:T(8,128)S(1)}, f32[1,3,2,256,256]{4,3,2,1,0:T(8,128)}, u32[]{:S(2)}) %copy-start.2) | copy-done | bytes 1572888
  6.6 0.0 copy-start.3
  6.6 1.4 %copy-done.3 = f32[1,3,2,256,256]{4,3,2,1,0:T(8,128)S(1)} copy-done((f32[1,3,2,256,256]{4,3,2,1,0:T(8,128)S(1)}, f32[1,3,2,256,256]{4,3,2,1,0:T(8,128)}, u32[]{:S(2)}) %copy-start.3) | copy-done | bytes 1572888
  8.1 0.0 copy-start.4
  8.1 0.7 %copy-done.4 = f32[1,3]{1,0:T(1,128)S(1)} copy-done((f32[1,3]{1,0:T(1,128)S(1)}, f32[1,3]{1,0:T(1,128)}, u32[]{:S(2)}) %copy-start.4) | copy-done | bytes 36
  8.7 0.0 copy-start.6
  8.7 1.2 %copy-done.6 = bf16[4,2,256,256]{3,2,1,0:T(8,128)(2,1)S(1)} copy-done((bf16[4,2,256,256]{3,2,1,0:T(8,128)(2,1)S(1)}, bf16[4,2,256,256]{3,2,1,0:T(8,128)(2,1)}, u32[]{:S(2)}) %copy-start.6) | copy-done | bytes 1048600
  9.9 0.0 copy-start.8
  9.9 0.9 %copy-done.8 = f32[256,256]{1,0:T(8,128)S(1)} copy-done((f32[256,256]{1,0:T(8,128)S(1)}, f32[256,256]{1,0:T(8,128)}, u32[]{:S(2)}) %copy-start.8) | copy-done | bytes 262168
  10.9 0.0 copy-start.10
  10.9 0.9 %copy-done.10 = f32[136,128]{1,0:T(8,128)S(1)} copy-done((f32[136,128]{1,0:T(8,128)S(1)}, f32[136,128]{1,0:T(8,128)}, u32[]{:S(2)}) %copy-start.10) | copy-done | bytes 69656
  11.8 0.0 copy-start.1
  11.8 0.0 copy-start.5
  11.8 0.0 copy-start.11
  11.8 6.5 %first_levels.1 = (bf16[2,2,2,256,256]{4,3,2,1,0:T(8,128)(2,1)S(1)}, f32[2,256,256]{2,1,0:T(8,128)S(1)}) custom-call(s32[3]{0:T(128)S(1)} %pad_add_fusion.1.who, f32[3]{0:T(128)S(1)} %bitcast.33, f32[3,2,256,256]{3,2,1,0:T(8,128)S(1)} %bitcast.28, f32[3,2,256,256]{3,2,1,0:T(8,128)S(1)} %bitcast.29, f32[2,256,256]{2,1,0:T(8,128)S(1)} %bitcast.25, ...), custom_call_target="tpu_custom_call" | custom-call | flops 8000000000 | bytes 10000000 | tf_op jit(solution)/shard_map/first_levels/pallas_call | solution.py:351
  18.3 0.0 copy-start.12
  18.4 1.0 %copy-done.12 = bf16[2,2,2,256,256]{4,3,2,1,0:T(8,128)(2,1)} copy-done((bf16[2,2,2,256,256]{4,3,2,1,0:T(8,128)(2,1)}, bf16[2,2,2,256,256]{4,3,2,1,0:T(8,128)(2,1)S(1)}, u32[]{:S(2)}) %copy-start.12) | copy-done | bytes 1048600
  19.3 0.1 stack.43.who
  19.4 0.0 collective-permute-done
  19.4 0.0 copy-done.1
  19.4 0.0 copy-done.5
  19.4 0.0 copy-done.7
  19.5 0.0 copy-done.9
  19.5 0.0 copy-done.11
  19.5 0.0 copy-start.13
  19.5 1.2 %copy-done.13 = bf16[2,2,2,256,256]{4,3,2,1,0:T(8,128)(2,1)S(1)} copy-done((bf16[2,2,2,256,256]{4,3,2,1,0:T(8,128)(2,1)S(1)}, bf16[2,2,2,256,256]{4,3,2,1,0:T(8,128)(2,1)}, u32[]{:S(2)}) %copy-start.13) | copy-done | bytes 1048600
  20.7 6.4 %other_levels.1 = (f32[2,256,128]{2,1,0:T(8,128)S(1)}, bf16[1,2,256,128]{3,2,1,0:T(8,128)(2,1)S(1)}, f32[1,2,256,128]{3,2,1,0:T(8,128)S(1)}, bf16[1,1,2,256,128]{4,3,2,1,0:T(8,128)(2,1)S(1)}) custom-call(s32[5]{0:T(128)S(1)} %stack.43.who, f32[3]{0:T(128)S(1)} %bitcast.34, bf16[2,2,2,256,256]{4,3,2,1,0:T(8,128)(2,1)S(1)} %copy-done.13, ...), custom_call_target="tpu_custom_call" | custom-call | flops 8000000000 | bytes 10000000 | tf_op jit(solution)/shard_map/other_levels/pallas_call | solution.py:364
  27.1 0.1 collective-permute-start.2
  27.8 0.1 pad_add_fusion.where
  27.9 0.5 %collective-permute-start.1 = (bf16[2,256,128]{2,1,0:T(8,128)(2,1)S(1)}, bf16[2,256,128]{2,1,0:T(8,128)(2,1)S(1)}, u32[]{:S(2)}, u32[]{:S(2)}) collective-permute-start(bf16[2,256,128]{2,1,0:T(8,128)(2,1)S(1)} %bitcast.31), channel_id=1, source_target_pairs={{0,1},{1,0},{2,3},{3,2},{4,5},{5,4},{6,7},{7,6},{8,9},{9,8},{10,11... | collective-permute-start | bytes 393224 | tf_op jit(solution)/shard_map/ppermute | solution.py:327
  28.4 0.1 collective-permute-done.2
  28.5 0.1 collective-permute-start.3
  28.6 0.8 %collective-permute-done.1 = bf16[2,256,128]{2,1,0:T(8,128)(2,1)S(1)} collective-permute-done((bf16[2,256,128]{2,1,0:T(8,128)(2,1)S(1)}, bf16[2,256,128]{2,1,0:T(8,128)(2,1)S(1)}, u32[]{:S(2)}, u32[]{:S(2)}) %collective-permute-start.1) | collective-permute-done | bytes 131104 | tf_op jit(solution)/shard_map/ppermute | solution.py:327
  29.4 4.7 %collective-permute-done.3 = bf16[2,256,128]{2,1,0:T(8,128)(2,1)S(1)} collective-permute-done((bf16[2,256,128]{2,1,0:T(8,128)(2,1)S(1)}, bf16[2,256,128]{2,1,0:T(8,128)(2,1)S(1)}, u32[]{:S(2)}, u32[]{:S(2)}) %collective-permute-start.3) | collective-permute-done | bytes 131104 | tf_op jit(solution)/shard_map/ppermute | solution.py:327
  34.1 0.7 %place.1 = bf16[4,2,128,128]{3,2,1,0:T(8,128)(2,1)S(1)} custom-call(s32[2]{0:T(128)S(1)} %pad_add_fusion.where, f32[2,256,128]{2,1,0:T(8,128)S(1)} %convert_add_fusion.own, bf16[1,2,256,128]{3,2,1,0:T(8,128)(2,1)S(1)} %bitcast.27), custom_call_target="tpu_custom_call" | custom-call | tf_op jit(solution)/shard_map/place/pallas_call | solution.py:386
  34.8 3.6 %collective-permute-start.6 = (bf16[2,128,128]{2,1,0:T(8,128)(2,1)S(1)}, bf16[2,128,128]{2,1,0:T(8,128)(2,1)S(1)}, u32[]{:S(2)}, u32[]{:S(2)}) collective-permute-start(bf16[2,128,128]{2,1,0:T(8,128)(2,1)S(1)} %get-tuple-element.17), channel_id=1, source_target_pairs={{0,12},{4,0},{8,4},{12,8},{1,13},{5,1},{9,5},{13,9},{2,14},{6,2},{... | collective-permute-start | bytes 196616 | tf_op jit(solution)/shard_map/ppermute | solution.py:327
  38.5 0.0 collective-permute-start.5
  38.5 1.0 %collective-permute-start.4 = (bf16[2,128,128]{2,1,0:T(8,128)(2,1)S(1)}, bf16[2,128,128]{2,1,0:T(8,128)(2,1)S(1)}, u32[]{:S(2)}, u32[]{:S(2)}) collective-permute-start(bf16[2,128,128]{2,1,0:T(8,128)(2,1)S(1)} %get-tuple-element.19), channel_id=1, source_target_pairs={{0,4},{4,8},{8,12},{12,0},{1,5},{5,9},{9,13},{13,1},{2,6},{6,10},{... | collective-permute-start | bytes 196616 | tf_op jit(solution)/shard_map/ppermute | solution.py:327
  39.5 1.2 %collective-permute-done.6.refs_3_ = bf16[2,128,128]{2,1,0:T(8,128)(2,1)S(1)} collective-permute-done((bf16[2,128,128]{2,1,0:T(8,128)(2,1)S(1)}, bf16[2,128,128]{2,1,0:T(8,128)(2,1)S(1)}, u32[]{:S(2)}, u32[]{:S(2)}) %collective-permute-start.6) | collective-permute-done | bytes 65568 | tf_op jit(solution)/shard_map/ppermute | solution.py:327
  40.7 3.1 %collective-permute-done.5.refs_2_ = bf16[2,128,128]{2,1,0:T(8,128)(2,1)S(1)} collective-permute-done((bf16[2,128,128]{2,1,0:T(8,128)(2,1)S(1)}, bf16[2,128,128]{2,1,0:T(8,128)(2,1)S(1)}, u32[]{:S(2)}, u32[]{:S(2)}) %collective-permute-start.5) | collective-permute-done | bytes 65568 | tf_op jit(solution)/shard_map/ppermute | solution.py:327
  43.8 0.8 %collective-permute-done.4.refs_1_ = bf16[2,128,128]{2,1,0:T(8,128)(2,1)S(1)} collective-permute-done((bf16[2,128,128]{2,1,0:T(8,128)(2,1)S(1)}, bf16[2,128,128]{2,1,0:T(8,128)(2,1)S(1)}, u32[]{:S(2)}, u32[]{:S(2)}) %collective-permute-start.4) | collective-permute-done | bytes 65568 | tf_op jit(solution)/shard_map/ppermute | solution.py:327
  44.6 0.7 %gather.1 = f32[128,2,128]{2,1,0:T(2,128)} custom-call(bf16[2,128,128]{2,1,0:T(8,128)(2,1)S(1)} %get-tuple-element.20.refs_0_, bf16[2,128,128]{2,1,0:T(8,128)(2,1)S(1)} %collective-permute-done.4.refs_1_, bf16[2,128,128]{2,1,0:T(8,128)(2,1)S(1)} %collective-permute-done.5.refs_2_, bf16[2,128,128]{2,1,0:T(8,128)(2,1)S(1)} %collective-permute-done.6.refs_3_), custom_call_target="tpu_custom_call" | custom-call | tf_op jit(solution)/shard_map/gather/pallas_call | solution.py:396
  (5 shorter events, 0.1 us)
Async XLA Ops:
  1.1 18.3 %collective-permute-start = (bf16[2,256,256]{2,1,0:T(8,128)(2,1)S(1)}, bf16[2,256,256]{2,1,0:T(8,128)(2,1)S(1)}, u32[]{:S(2)}, u32[]{:S(2)}) collective-permute-start(bf16[2,256,256]{2,1,0:T(8,128)(2,1)S(1)} %add_convert_fusion), channel_id=1, source_target_pairs={{0,2},{2,0},{1,3},{3,1},{4,6},{6,4},{5,7},{7,5},{8,10},{10,8},{9,1... | collective-permute-start | bytes 786440 | tf_op jit(solution)/shard_map/ppermute | solution.py:327
  4.2 1.0 %copy-start = (f32[1,2,256,256]{3,2,1,0:T(8,128)S(1)}, f32[1,2,256,256]{3,2,1,0:T(8,128)}, u32[]{:S(2)}) copy-start(f32[1,2,256,256]{3,2,1,0:T(8,128)} %param.10) | copy-start | bytes 1572868
  5.2 1.4 %copy-start.2 = (f32[1,3,2,256,256]{4,3,2,1,0:T(8,128)S(1)}, f32[1,3,2,256,256]{4,3,2,1,0:T(8,128)}, u32[]{:S(2)}) copy-start(f32[1,3,2,256,256]{4,3,2,1,0:T(8,128)} %param.8) | copy-start | bytes 4718596
  6.6 1.4 %copy-start.3 = (f32[1,3,2,256,256]{4,3,2,1,0:T(8,128)S(1)}, f32[1,3,2,256,256]{4,3,2,1,0:T(8,128)}, u32[]{:S(2)}) copy-start(f32[1,3,2,256,256]{4,3,2,1,0:T(8,128)} %param.9) | copy-start | bytes 4718596
  8.1 0.7 %copy-start.4 = (f32[1,3]{1,0:T(1,128)S(1)}, f32[1,3]{1,0:T(1,128)}, u32[]{:S(2)}) copy-start(f32[1,3]{1,0:T(1,128)} %param.11) | copy-start | bytes 40
  8.7 1.2 %copy-start.6 = (bf16[4,2,256,256]{3,2,1,0:T(8,128)(2,1)S(1)}, bf16[4,2,256,256]{3,2,1,0:T(8,128)(2,1)}, u32[]{:S(2)}) copy-start(bf16[4,2,256,256]{3,2,1,0:T(8,128)(2,1)} %constant.26.clone.T) | copy-start | bytes 3145732
  9.9 0.9 %copy-start.8 = (f32[256,256]{1,0:T(8,128)S(1)}, f32[256,256]{1,0:T(8,128)}, u32[]{:S(2)}) copy-start(f32[256,256]{1,0:T(8,128)} %constant.28.clone.win) | copy-start | bytes 786436
  10.9 0.9 %copy-start.10 = (f32[136,128]{1,0:T(8,128)S(1)}, f32[136,128]{1,0:T(8,128)}, u32[]{:S(2)}) copy-start(f32[136,128]{1,0:T(8,128)} %constant.27.clone.K2) | copy-start | bytes 208900
  11.8 7.7 %copy-start.1 = (f32[1,2,256,256]{3,2,1,0:T(8,128)S(1)}, f32[1,2,256,256]{3,2,1,0:T(8,128)}, u32[]{:S(2)}) copy-start(f32[1,2,256,256]{3,2,1,0:T(8,128)} %param.10) | copy-start | bytes 1572868
  11.8 7.7 %copy-start.5 = (f32[1,3]{1,0:T(1,128)S(1)}, f32[1,3]{1,0:T(1,128)}, u32[]{:S(2)}) copy-start(f32[1,3]{1,0:T(1,128)} %param.11) | copy-start | bytes 40
  11.8 7.7 %copy-start.7 = (bf16[4,2,256,256]{3,2,1,0:T(8,128)(2,1)S(1)}, bf16[4,2,256,256]{3,2,1,0:T(8,128)(2,1)}, u32[]{:S(2)}) copy-start(bf16[4,2,256,256]{3,2,1,0:T(8,128)(2,1)} %constant.26.clone.T) | copy-start | bytes 3145732
  11.8 7.7 %copy-start.9 = (f32[256,256]{1,0:T(8,128)S(1)}, f32[256,256]{1,0:T(8,128)}, u32[]{:S(2)}) copy-start(f32[256,256]{1,0:T(8,128)} %constant.28.clone.win) | copy-start | bytes 786436
  11.8 7.7 %copy-start.11 = (f32[136,128]{1,0:T(8,128)S(1)}, f32[136,128]{1,0:T(8,128)}, u32[]{:S(2)}) copy-start(f32[136,128]{1,0:T(8,128)} %constant.27.clone.K2) | copy-start | bytes 208900
  18.3 1.0 %copy-start.12 = (bf16[2,2,2,256,256]{4,3,2,1,0:T(8,128)(2,1)}, bf16[2,2,2,256,256]{4,3,2,1,0:T(8,128)(2,1)S(1)}, u32[]{:S(2)}) copy-start(bf16[2,2,2,256,256]{4,3,2,1,0:T(8,128)(2,1)S(1)} %get-tuple-element.11.st_in) | copy-start | bytes 3145732
  19.5 1.2 %copy-start.13 = (bf16[2,2,2,256,256]{4,3,2,1,0:T(8,128)(2,1)S(1)}, bf16[2,2,2,256,256]{4,3,2,1,0:T(8,128)(2,1)}, u32[]{:S(2)}) copy-start(bf16[2,2,2,256,256]{4,3,2,1,0:T(8,128)(2,1)} %copy-done.12) | copy-start | bytes 3145732
  27.1 1.4 %collective-permute-start.2 = (bf16[1,2,256,128]{3,2,1,0:T(8,128)(2,1)S(1)}, bf16[1,2,256,128]{3,2,1,0:T(8,128)(2,1)S(1)}, u32[]{:S(2)}, u32[]{:S(2)}) collective-permute-start(bf16[1,2,256,128]{3,2,1,0:T(8,128)(2,1)S(1)} %bitcast.32), channel_id=1, source_target_pairs={{0,1},{1,0},{2,3},{3,2},{4,5},{5,4},{6,7},{7,6},{8,9},{9,8},{10,11... | collective-permute-start | bytes 393224 | tf_op jit(solution)/shard_map/ppermute | solution.py:327
  27.9 1.5 %collective-permute-start.1 = (bf16[2,256,128]{2,1,0:T(8,128)(2,1)S(1)}, bf16[2,256,128]{2,1,0:T(8,128)(2,1)S(1)}, u32[]{:S(2)}, u32[]{:S(2)}) collective-permute-start(bf16[2,256,128]{2,1,0:T(8,128)(2,1)S(1)} %bitcast.31), channel_id=1, source_target_pairs={{0,1},{1,0},{2,3},{3,2},{4,5},{5,4},{6,7},{7,6},{8,9},{9,8},{10,11... | collective-permute-start | bytes 393224 | tf_op jit(solution)/shard_map/ppermute | solution.py:327
  28.5 5.6 %collective-permute-start.3 = (bf16[2,256,128]{2,1,0:T(8,128)(2,1)S(1)}, bf16[2,256,128]{2,1,0:T(8,128)(2,1)S(1)}, u32[]{:S(2)}, u32[]{:S(2)}) collective-permute-start(bf16[2,256,128]{2,1,0:T(8,128)(2,1)S(1)} %fusion), channel_id=1, source_target_pairs={{0,2},{2,0},{1,3},{3,1},{4,6},{6,4},{5,7},{7,5},{8,10},{10,8},{9,1... | collective-permute-start | bytes 393224 | tf_op jit(solution)/shard_map/ppermute | solution.py:327
  34.8 5.9 %collective-permute-start.6 = (bf16[2,128,128]{2,1,0:T(8,128)(2,1)S(1)}, bf16[2,128,128]{2,1,0:T(8,128)(2,1)S(1)}, u32[]{:S(2)}, u32[]{:S(2)}) collective-permute-start(bf16[2,128,128]{2,1,0:T(8,128)(2,1)S(1)} %get-tuple-element.17), channel_id=1, source_target_pairs={{0,12},{4,0},{8,4},{12,8},{1,13},{5,1},{9,5},{13,9},{2,14},{6,2},{... | collective-permute-start | bytes 196616 | tf_op jit(solution)/shard_map/ppermute | solution.py:327
  38.5 5.3 %collective-permute-start.5 = (bf16[2,128,128]{2,1,0:T(8,128)(2,1)S(1)}, bf16[2,128,128]{2,1,0:T(8,128)(2,1)S(1)}, u32[]{:S(2)}, u32[]{:S(2)}) collective-permute-start(bf16[2,128,128]{2,1,0:T(8,128)(2,1)S(1)} %get-tuple-element.18), channel_id=1, source_target_pairs={{0,8},{4,12},{8,0},{12,4},{1,9},{5,13},{9,1},{13,5},{2,10},{6,14},... | collective-permute-start | bytes 196616 | tf_op jit(solution)/shard_map/ppermute | solution.py:327
  38.5 6.1 %collective-permute-start.4 = (bf16[2,128,128]{2,1,0:T(8,128)(2,1)S(1)}, bf16[2,128,128]{2,1,0:T(8,128)(2,1)S(1)}, u32[]{:S(2)}, u32[]{:S(2)}) collective-permute-start(bf16[2,128,128]{2,1,0:T(8,128)(2,1)S(1)} %get-tuple-element.19), channel_id=1, source_target_pairs={{0,4},{4,8},{8,12},{12,0},{1,5},{5,9},{9,13},{13,1},{2,6},{6,10},{... | collective-permute-start | bytes 196616 | tf_op jit(solution)/shard_map/ppermute | solution.py:327

commit v2 on v1

--- a/solution.py
+++ b/solution.py
@@ -183,7 +183,7 @@
     st_ab[1] = jnp.concatenate([src[0, :, :h] - src[0, :, h:], src[1, :, :h] - src[1, :, h:]], axis=1).astype(bf)
 
 
-ANY = pl.BlockSpec(memory_space=pl.ANY)
+HBM = pl.BlockSpec(memory_space=pltpu.HBM)
 VM = pl.BlockSpec(memory_space=pltpu.VMEM)
 SM = pl.BlockSpec(memory_space=pltpu.SMEM)
 F32, BF16 = jnp.float32, jnp.bfloat16
@@ -193,53 +193,62 @@
     return pltpu.CompilerParams(vmem_limit_bytes=mib * 1024 * 1024)
 
 
-def first_levels(dims, who, om, src, rcv, slow, T, K2, win, st_out, own_out, raw, st, P, c, D, sem_in, sem_out):
-    n, slots, L = dims
-    nf, f0, levels = who[0], who[1], who[2]
+def share(fronts, depth):
+    d = lax.axis_index("depth")
+    base, extra = fronts // depth, fronts % depth
+    return d, base + jnp.where(d < extra, 1, 0), d * base + jnp.minimum(d, extra)
+
+
+def first_levels(dims, om_h, src, rcv, slow_h, T_h, K2_h, win_h, st, own_out,
+                 om, raw, slow, T, K2, win, P, c, D, sem_in, sem_t):
+    n, slots, L, fronts, depth = dims
+    d, nf, f0 = share(fronts, depth)
 
     def moves(j):
-        fr = f0 + j
+        fr = jnp.minimum(f0 + j, fronts - 1)
         return (
             pltpu.make_async_copy(src.at[fr], raw.at[j, 0], sem_in.at[j, 0]),
             pltpu.make_async_copy(rcv.at[fr], raw.at[j, 1], sem_in.at[j, 1]),
         )
 
+    tables = [
+        pltpu.make_async_copy(a, b, sem_t.at[i])
+        for i, (a, b) in enumerate(((om_h, om), (slow_h, slow), (T_h, T), (K2_h, K2), (win_h, win)))
+    ]
     for j in range(slots):
-        @pl.when(j < nf)
-        def _(j=j):
-            for m in moves(j):
+        for m in moves(j):
+            m.start()
+        if j == 0:
+            for m in tables:
                 m.start()
     for j in range(slots):
-        @pl.when(j < nf)
-        def _(j=j):
-            for f, m in enumerate(moves(j)):
-                m.wait()
-                prep(n, raw.at[j, f], st.at[j, f])
+        for f, m in enumerate(moves(j)):
+            m.wait()
+            prep(n, raw.at[j, f], st.at[j, f])
+    for m in tables:
+        m.wait()
 
     def level(z, _):
         s0 = level_prep(n, slow.at[z], win, D)
         own_out[z] = jnp.zeros((n, n), F32)
 
         def front(j, _):
-            front_math(n, om[f0 + j], s0, T, K2, win, st.at[j], own_out.at[z], P, c, D)
+            front_math(n, om[0, f0 + j], s0, T, K2, win, st.at[j], own_out.at[z], P, c, D)
             return 0
 
         lax.fori_loop(0, nf, front, 0)
         return 0
 
-    lax.fori_loop(0, levels, level, 0)
-    out = pltpu.make_async_copy(st, st_out, sem_out)
-    out.start()
-    out.wait()
-
-
-def other_levels(dims, who, om, st_in, slow, got, own_in, T, K2, win, keep_own, send_own, keep_oth, send_oth,
-                 st, s_now, part, P, c, D, sem):
-    n, L, depth, freq = dims
-    nf, f0, lo, d, fq = who[0], who[1], who[2], who[3], who[4]
+    lax.fori_loop(0, jnp.where(d == 0, L, 0), level, 0)
+
+
+def other_levels(dims, om, st_in, slow, got, own_in, T, K2, win, keep_own, send_own, keep_oth, send_oth, st,
+                 s_now, part, P, c, D):
+    n, L, fronts, depth, freq = dims
+    d, nf, f0 = share(fronts, depth)
+    fq = lax.axis_index("freq")
+    lo = jnp.where(d == 0, L, 0)
     w = n // freq
-    move = pltpu.make_async_copy(st_in, st, sem)
-    move.start()
 
     def split(ref, keep, sends):
         for a in range(freq):
@@ -255,8 +264,6 @@
         for z in range(L):
             split(own_in.at[z], keep_own.at[z], send_own.at[:, z])
 
-    move.wait()
-
     def level(z, _):
         owner = z // L
         zl = z - owner * L
@@ -274,7 +281,7 @@
         part[...] = jnp.zeros((n, n), F32)
 
         def front(j, _):
-            front_math(n, om[f0 + j], s0, T, K2, win, st.at[j], part, P, c, D)
+            front_math(n, om[0, f0 + j], s0, T, K2, win, st.at[j], part, P, c, D)
             return 0
 
         lax.fori_loop(0, nf, front, 0)
@@ -293,11 +300,11 @@
     lax.fori_loop(lo, depth * L, level, 0)
 
 
-def place(dims, where, own, got, out, padded):
+def place(dims, start, own, got, out, padded):
     n, L, shots, more = dims
     w = own.shape[-1]
     survey = shots * TILE
-    me, begin = where[0], where[1]
+    me, begin = lax.axis_index("shot"), start[0]
     padded[:, :survey] = jnp.zeros((L, survey, w), F32)
     padded[:, survey + n:] = jnp.zeros((L, survey, w), F32)
     for z in range(L):
@@ -332,47 +339,43 @@
     h = n // 2
     fronts, L = source.shape[1], slowness.shape[1]
     depth, freq, shots = lax.axis_size("depth"), lax.axis_size("freq"), lax.axis_size("shot")
-    d, fq, me = lax.axis_index("depth"), lax.axis_index("freq"), lax.axis_index("shot")
     T, K2, win = make_tables(n)
     slots = -(-fronts // depth)
-    base, extra = fronts // depth, fronts % depth
-    nf = base + jnp.where(d < extra, 1, 0)
-    f0 = d * base + jnp.minimum(d, extra)
     w = n // freq
     S = jax.ShapeDtypeStruct
     V = pltpu.VMEM
-    om, slow = omegas[0], slowness[0]
+    slow = slowness[0]
 
     sent = (slow - 1.0).astype(BF16)
     got = jnp.stack([shift(sent, "depth", r) for r in range(1, depth)])
 
     math_scratch = [V((2, h + 8, n), F32), V((2, n, n), F32), V((2, n, n), F32)]
-    who = jnp.stack([nf, f0, jnp.where(d == 0, L, 0)]).astype(jnp.int32)
     state, own_a = pl.pallas_call(
-        functools.partial(first_levels, (n, slots, L)),
+        functools.partial(first_levels, (n, slots, L, fronts, depth)),
         out_shape=(S((slots, 2, 2, n, n), BF16), S((L, n, n), F32)),
-        in_specs=[SM, SM, ANY, ANY, VM, VM, VM, VM],
-        out_specs=(ANY, VM),
-        scratch_shapes=[V((slots, 2, 2, n, n), F32), V((slots, 2, 2, n, n), BF16)] + math_scratch
-        + [pltpu.SemaphoreType.DMA((slots, 2)), pltpu.SemaphoreType.DMA],
-        compiler_params=params(32),
+        in_specs=[HBM] * 7,
+        out_specs=(VM, VM),
+        scratch_shapes=[pltpu.SMEM((1, fronts), F32), V((slots, 2, 2, n, n), F32), V((L, n, n), F32),
+                        V((4, 2, n, n), BF16), V((h + 8, h), F32), V((n, n), F32)] + math_scratch
+        + [pltpu.SemaphoreType.DMA((slots, 2)), pltpu.SemaphoreType.DMA((5,))],
+        compiler_params=params(50),
         cost_estimate=pl.CostEstimate(flops=8 * 10**9, bytes_accessed=10**7, transcendentals=10**6),
         name="first_levels",
-    )(who, om, source[0], receiver[0], slow, T, K2, win)
-
-    who = jnp.stack([nf, f0, jnp.where(d == 0, L, 0), d, fq]).astype(jnp.int32)
-    keep_own, send_own, keep_oth, send_oth = pl.pallas_call(
-        functools.partial(other_levels, (n, L, depth, freq)),
+    )(omegas, source[0], receiver[0], slow, T, K2, win)
+
+    keep_own, send_own, keep_oth, send_oth, _ = pl.pallas_call(
+        functools.partial(other_levels, (n, L, fronts, depth, freq)),
         out_shape=(S((L, n, w), F32), S((freq - 1, L, n, w), BF16),
-                   S((depth - 1, L, n, w), F32), S((freq - 1, depth - 1, L, n, w), BF16)),
-        in_specs=[SM, SM, ANY, VM, VM, VM, VM, VM, VM],
-        out_specs=(VM, VM, VM, VM),
-        scratch_shapes=[V((slots, 2, 2, n, n), BF16), V((n, n), F32), V((n, n), F32)] + math_scratch
-        + [pltpu.SemaphoreType.DMA],
+                   S((depth - 1, L, n, w), F32), S((freq - 1, depth - 1, L, n, w), BF16),
+                   S(state.shape, state.dtype)),
+        in_specs=[SM, VM, VM, VM, VM, VM, VM, VM],
+        out_specs=(VM, VM, VM, VM, VM),
+        input_output_aliases={1: 4},
+        scratch_shapes=[V((n, n), F32), V((n, n), F32)] + math_scratch,
         compiler_params=params(32),
         cost_estimate=pl.CostEstimate(flops=8 * 10**9, bytes_accessed=10**7, transcendentals=10**6),
         name="other_levels",
-    )(who, om, state, slow, got, own_a, T, K2, win)
+    )(omegas, state, slow, got, own_a, T, K2, win)
 
     own, oth = keep_own, keep_oth
     for r in range(1, freq):
@@ -382,7 +385,6 @@
     oth = oth.astype(BF16)
     arrived = jnp.stack([shift(oth[r - 1], "depth", r) for r in range(1, depth)])
 
-    where = jnp.stack([me, shot_start[0]]).astype(jnp.int32)
     blocks = pl.pallas_call(
         functools.partial(place, (n, L, shots, depth - 1)),
         out_shape=S((shots, L, TILE, w), BF16),
@@ -391,7 +393,7 @@
         scratch_shapes=[V((L, 2 * shots * TILE + n, w), F32)],
         compiler_params=params(32),
         name="place",
-    )(where, own, arrived)
+    )(shot_start, own, arrived)
     pieces = [blocks[0]] + [shift(blocks[r], "shot", r) for r in range(1, shots)]
     return pl.pallas_call(
         functools.partial(gather, (L, shots)),

time: 45.7 us -> 39.5 us (0.86)
  local copies, waits for them, and re-layouts: 9.9 us -> 4.77 us
  waiting for transfers between devices: 10.7 us -> 8.94 us
  starting transfers between devices: 8.34 us -> 9.31 us
    unnamed x28 -> x10, local copies, waits for them, and re-layouts: 9.8 us -> 4.75 us
    ppermute x7, waiting for transfers between devices: 10.7 us -> 8.94 us  [shift(): lax.ppermute(array, axis, [(i, (i + by) % size) for i in range(size)])]
    ppermute x7, starting transfers between devices: 8.34 us -> 9.31 us  [shift(): lax.ppermute(array, axis, [(i, (i + by) % size) for i in range(size)])]
    pallas_call x1, Pallas kernels: 0.65 us -> 0.11 us  [local(): pl.pallas_call(functools.partial(place, (n, L, shots, depth - 1)), out_sh...]
    pallas_call x2, Pallas kernels: 12.9 us -> 13.4 us  [the longest x1 7.23 us: local(): pl.pallas_call(functools.partial(first_levels, (n, slots, L, fronts, dept...]
  transfers between devices with their start and end apart: 7 -> 7, of which waited for: 6 -> 6; matrix products, arithmetic and copies ran while one was open for 1% -> 0% of each run, Pallas kernels for 14% -> 18%
where the time goes in v2:
time: 39.5 us; the launch traced here: 39.2 us
  Pallas kernels  14.3 us (36%)
  starting transfers between devices  9.31 us (24%)
  waiting for transfers between devices  8.94 us (23%)
  local copies, waits for them, and re-layouts  4.77 us (12%)
  other arithmetic  1.14 us (3%)
  between operations  0.72 us (2%)
    ppermute x7, starting transfers between devices, shift(): lax.ppermute(array, axis, [(i, (i + by) % size) for i in range(size)])  9.31 us
    ppermute x7, waiting for transfers between devices, shift(): lax.ppermute(array, axis, [(i, (i + by) % size) for i in range(size)])  8.94 us
    pallas_call x1, Pallas kernels, local(): pl.pallas_call(functools.partial(first_levels, (n, slots, L, fronts, dept...  7.23 us
    pallas_call x1, Pallas kernels, local(): pl.pallas_call(functools.partial(other_levels, (n, L, fronts, depth, freq...  6.19 us
    unnamed x10, local copies, waits for them, and re-layouts  4.75 us
    convert_element_type x1, other arithmetic, local(): sent = (slow - 1.0).astype(BF16)  1.08 us
  transfers between devices with their start and end apart: 7, of which 6 were waited for; matrix products, arithmetic and copies ran while one was open for 0% of the time, Pallas kernels for 18%

profile of v2, /device:TPU:0, one launch (start us, length us, event | category | flops | bytes accessed | tf_op | source)
XLA Modules:
  0.0 39.2 jit_solution(1251757616675858552)
XLA Ops:
  0.0 1.1 %add_convert_fusion = bf16[2,256,256]{2,1,0:T(8,128)(2,1)S(1)} fusion(f32[1,2,256,256]{3,2,1,0:T(8,128)} %param.10), kind=kLoop, calls=%fused_computation | loop fusion | flops 262144 | bytes 786432 | tf_op jit(solution)/shard_map/convert_element_type | solution.py:349
  1.1 3.0 %collective-permute-start = (bf16[2,256,256]{2,1,0:T(8,128)(2,1)S(1)}, bf16[2,256,256]{2,1,0:T(8,128)(2,1)S(1)}, u32[]{:S(2)}, u32[]{:S(2)}) collective-permute-start(bf16[2,256,256]{2,1,0:T(8,128)(2,1)S(1)} %add_convert_fusion), channel_id=1, source_target_pairs={{0,2},{2,0},{1,3},{3,1},{4,6},{6,4},{5,7},{7,5},{8,10},{10,8},{9,1... | collective-permute-start | bytes 786440 | tf_op jit(solution)/shard_map/ppermute | solution.py:334
  4.1 0.0 copy-start
  4.1 1.0 %copy-done = f32[1,2,256,256]{3,2,1,0:T(8,128)S(1)} copy-done((f32[1,2,256,256]{3,2,1,0:T(8,128)S(1)}, f32[1,2,256,256]{3,2,1,0:T(8,128)}, u32[]{:S(2)}) %copy-start) | copy-done | bytes 524312
  5.2 0.0 copy-start.1
  5.2 0.7 %copy-done.1 = f32[1,3]{1,0:T(1,128)S(1)} copy-done((f32[1,3]{1,0:T(1,128)S(1)}, f32[1,3]{1,0:T(1,128)}, u32[]{:S(2)}) %copy-start.1) | copy-done | bytes 36
  5.8 0.0 copy-start.2
  5.8 1.2 %copy-done.2 = bf16[4,2,256,256]{3,2,1,0:T(8,128)(2,1)S(1)} copy-done((bf16[4,2,256,256]{3,2,1,0:T(8,128)(2,1)S(1)}, bf16[4,2,256,256]{3,2,1,0:T(8,128)(2,1)}, u32[]{:S(2)}) %copy-start.2) | copy-done | bytes 1048600
  7.0 0.0 copy-start.3
  7.0 0.9 %copy-done.3 = f32[256,256]{1,0:T(8,128)S(1)} copy-done((f32[256,256]{1,0:T(8,128)S(1)}, f32[256,256]{1,0:T(8,128)}, u32[]{:S(2)}) %copy-start.3) | copy-done | bytes 262168
  8.0 0.0 copy-start.4
  8.0 0.9 %copy-done.4 = f32[136,128]{1,0:T(8,128)S(1)} copy-done((f32[136,128]{1,0:T(8,128)S(1)}, f32[136,128]{1,0:T(8,128)}, u32[]{:S(2)}) %copy-start.4) | copy-done | bytes 69656
  8.9 7.2 %first_levels.1 = (bf16[2,2,2,256,256]{4,3,2,1,0:T(8,128)(2,1)S(1)}, f32[2,256,256]{2,1,0:T(8,128)S(1)}) custom-call(f32[1,3]{1,0:T(1,128)S(1)} %copy-done.1, f32[3,2,256,256]{3,2,1,0:T(8,128)} %bitcast.24, f32[3,2,256,256]{3,2,1,0:T(8,128)} %bitcast.25, f32[2,256,256]{2,1,0:T(8,128)S(1)} %bitcast.18, bf16[4,2,256,256]{3,2,1,0:T(8,128)(2,1)S(1)} %copy-done.2, ...), custom_call_target="tpu_custom_call" | custom-call | flops 8000000000 | bytes 10000000 | tf_op jit(solution)/shard_map/first_levels/pallas_call | solution.py:353
  16.1 0.0 collective-permute-done
  16.1 6.2 %other_levels.1 = (f32[2,256,128]{2,1,0:T(8,128)S(1)}, bf16[1,2,256,128]{3,2,1,0:T(8,128)(2,1)S(1)}, f32[1,2,256,128]{3,2,1,0:T(8,128)S(1)}, bf16[1,1,2,256,128]...) custom-call(f32[1,3]{1,0:T(1,128)S(1)} %copy-done.1, ...), custom_call_target="tpu_custom_call", output_to_operand_aliasing={{4}: (1, {})} | custom-call | flops 8000000000 | bytes 10000000 | tf_op jit(solution)/shard_map/other_levels/pallas_call | solution.py:366
  22.3 0.1 collective-permute-start.2
  23.0 0.6 %collective-permute-start.1 = (bf16[2,256,128]{2,1,0:T(8,128)(2,1)S(1)}, bf16[2,256,128]{2,1,0:T(8,128)(2,1)S(1)}, u32[]{:S(2)}, u32[]{:S(2)}) collective-permute-start(bf16[2,256,128]{2,1,0:T(8,128)(2,1)S(1)} %bitcast.22), channel_id=1, source_target_pairs={{0,1},{1,0},{2,3},{3,2},{4,5},{5,4},{6,7},{7,6},{8,9},{9,8},{10,11... | collective-permute-start | bytes 393224 | tf_op jit(solution)/shard_map/ppermute | solution.py:334
  23.6 0.1 collective-permute-done.2
  23.8 0.1 collective-permute-start.3
  23.9 0.7 %collective-permute-done.1 = bf16[2,256,128]{2,1,0:T(8,128)(2,1)S(1)} collective-permute-done((bf16[2,256,128]{2,1,0:T(8,128)(2,1)S(1)}, bf16[2,256,128]{2,1,0:T(8,128)(2,1)S(1)}, u32[]{:S(2)}, u32[]{:S(2)}) %collective-permute-start.1) | collective-permute-done | bytes 131104 | tf_op jit(solution)/shard_map/ppermute | solution.py:334
  24.6 4.8 %collective-permute-done.3 = bf16[2,256,128]{2,1,0:T(8,128)(2,1)S(1)} collective-permute-done((bf16[2,256,128]{2,1,0:T(8,128)(2,1)S(1)}, bf16[2,256,128]{2,1,0:T(8,128)(2,1)S(1)}, u32[]{:S(2)}, u32[]{:S(2)}) %collective-permute-start.3) | collective-permute-done | bytes 131104 | tf_op jit(solution)/shard_map/ppermute | solution.py:334
  29.4 0.1 place.1
  29.5 1.6 %collective-permute-start.4 = (bf16[2,128,128]{2,1,0:T(8,128)(2,1)S(1)}, bf16[2,128,128]{2,1,0:T(8,128)(2,1)S(1)}, u32[]{:S(2)}, u32[]{:S(2)}) collective-permute-start(bf16[2,128,128]{2,1,0:T(8,128)(2,1)S(1)} %get-tuple-element.19), channel_id=1, source_target_pairs={{0,4},{4,8},{8,12},{12,0},{1,5},{5,9},{9,13},{13,1},{2,6},{6,10},{... | collective-permute-start | bytes 196616 | tf_op jit(solution)/shard_map/ppermute | solution.py:334
  31.2 2.6 %collective-permute-start.5 = (bf16[2,128,128]{2,1,0:T(8,128)(2,1)S(1)}, bf16[2,128,128]{2,1,0:T(8,128)(2,1)S(1)}, u32[]{:S(2)}, u32[]{:S(2)}) collective-permute-start(bf16[2,128,128]{2,1,0:T(8,128)(2,1)S(1)} %get-tuple-element.18), channel_id=1, source_target_pairs={{0,8},{4,12},{8,0},{12,4},{1,9},{5,13},{9,1},{13,5},{2,10},{6,14},... | collective-permute-start | bytes 196616 | tf_op jit(solution)/shard_map/ppermute | solution.py:334
  33.7 1.4 %collective-permute-start.6 = (bf16[2,128,128]{2,1,0:T(8,128)(2,1)S(1)}, bf16[2,128,128]{2,1,0:T(8,128)(2,1)S(1)}, u32[]{:S(2)}, u32[]{:S(2)}) collective-permute-start(bf16[2,128,128]{2,1,0:T(8,128)(2,1)S(1)} %get-tuple-element.17), channel_id=1, source_target_pairs={{0,12},{4,0},{8,4},{12,8},{1,13},{5,1},{9,5},{13,9},{2,14},{6,2},{... | collective-permute-start | bytes 196616 | tf_op jit(solution)/shard_map/ppermute | solution.py:334
  35.1 1.3 %collective-permute-done.4.refs_1_ = bf16[2,128,128]{2,1,0:T(8,128)(2,1)S(1)} collective-permute-done((bf16[2,128,128]{2,1,0:T(8,128)(2,1)S(1)}, bf16[2,128,128]{2,1,0:T(8,128)(2,1)S(1)}, u32[]{:S(2)}, u32[]{:S(2)}) %collective-permute-start.4) | collective-permute-done | bytes 65568 | tf_op jit(solution)/shard_map/ppermute | solution.py:334
  36.4 2.0 %collective-permute-done.5.refs_2_ = bf16[2,128,128]{2,1,0:T(8,128)(2,1)S(1)} collective-permute-done((bf16[2,128,128]{2,1,0:T(8,128)(2,1)S(1)}, bf16[2,128,128]{2,1,0:T(8,128)(2,1)S(1)}, u32[]{:S(2)}, u32[]{:S(2)}) %collective-permute-start.5) | collective-permute-done | bytes 65568 | tf_op jit(solution)/shard_map/ppermute | solution.py:334
  38.4 0.1 collective-permute-done.6.refs_3_
  38.4 0.7 %gather.1 = f32[128,2,128]{2,1,0:T(2,128)} custom-call(bf16[2,128,128]{2,1,0:T(8,128)(2,1)S(1)} %get-tuple-element.20.refs_0_, bf16[2,128,128]{2,1,0:T(8,128)(2,1)S(1)} %collective-permute-done.4.refs_1_, bf16[2,128,128]{2,1,0:T(8,128)(2,1)S(1)} %collective-permute-done.5.refs_2_, bf16[2,128,128]{2,1,0:T(8,128)(2,1)S(1)} %collective-permute-done.6.refs_3_), custom_call_target="tpu_custom_call" | custom-call | tf_op jit(solution)/shard_map/gather/pallas_call | solution.py:398
  (3 shorter events, 0.1 us)
Async XLA Ops:
  1.1 15.0 %collective-permute-start = (bf16[2,256,256]{2,1,0:T(8,128)(2,1)S(1)}, bf16[2,256,256]{2,1,0:T(8,128)(2,1)S(1)}, u32[]{:S(2)}, u32[]{:S(2)}) collective-permute-start(bf16[2,256,256]{2,1,0:T(8,128)(2,1)S(1)} %add_convert_fusion), channel_id=1, source_target_pairs={{0,2},{2,0},{1,3},{3,1},{4,6},{6,4},{5,7},{7,5},{8,10},{10,8},{9,1... | collective-permute-start | bytes 786440 | tf_op jit(solution)/shard_map/ppermute | solution.py:334
  4.1 1.0 %copy-start = (f32[1,2,256,256]{3,2,1,0:T(8,128)S(1)}, f32[1,2,256,256]{3,2,1,0:T(8,128)}, u32[]{:S(2)}) copy-start(f32[1,2,256,256]{3,2,1,0:T(8,128)} %param.10) | copy-start | bytes 1572868
  5.2 0.7 %copy-start.1 = (f32[1,3]{1,0:T(1,128)S(1)}, f32[1,3]{1,0:T(1,128)}, u32[]{:S(2)}) copy-start(f32[1,3]{1,0:T(1,128)} %om.1) | copy-start | bytes 40
  5.8 1.2 %copy-start.2 = (bf16[4,2,256,256]{3,2,1,0:T(8,128)(2,1)S(1)}, bf16[4,2,256,256]{3,2,1,0:T(8,128)(2,1)}, u32[]{:S(2)}) copy-start(bf16[4,2,256,256]{3,2,1,0:T(8,128)(2,1)} %constant.9.clone.T_h.T) | copy-start | bytes 3145732
  7.0 0.9 %copy-start.3 = (f32[256,256]{1,0:T(8,128)S(1)}, f32[256,256]{1,0:T(8,128)}, u32[]{:S(2)}) copy-start(f32[256,256]{1,0:T(8,128)} %constant.11.clone.win_h.win) | copy-start | bytes 786436
  8.0 0.9 %copy-start.4 = (f32[136,128]{1,0:T(8,128)S(1)}, f32[136,128]{1,0:T(8,128)}, u32[]{:S(2)}) copy-start(f32[136,128]{1,0:T(8,128)} %constant.10.clone.K2_h.K2) | copy-start | bytes 208900
  22.3 1.4 %collective-permute-start.2 = (bf16[1,2,256,128]{3,2,1,0:T(8,128)(2,1)S(1)}, bf16[1,2,256,128]{3,2,1,0:T(8,128)(2,1)S(1)}, u32[]{:S(2)}, u32[]{:S(2)}) collective-permute-start(bf16[1,2,256,128]{3,2,1,0:T(8,128)(2,1)S(1)} %bitcast.23), channel_id=1, source_target_pairs={{0,1},{1,0},{2,3},{3,2},{4,5},{5,4},{6,7},{7,6},{8,9},{9,8},{10,11... | collective-permute-start | bytes 393224 | tf_op jit(solution)/shard_map/ppermute | solution.py:334
  23.0 1.6 %collective-permute-start.1 = (bf16[2,256,128]{2,1,0:T(8,128)(2,1)S(1)}, bf16[2,256,128]{2,1,0:T(8,128)(2,1)S(1)}, u32[]{:S(2)}, u32[]{:S(2)}) collective-permute-start(bf16[2,256,128]{2,1,0:T(8,128)(2,1)S(1)} %bitcast.22), channel_id=1, source_target_pairs={{0,1},{1,0},{2,3},{3,2},{4,5},{5,4},{6,7},{7,6},{8,9},{9,8},{10,11... | collective-permute-start | bytes 393224 | tf_op jit(solution)/shard_map/ppermute | solution.py:334
  23.8 5.6 %collective-permute-start.3 = (bf16[2,256,128]{2,1,0:T(8,128)(2,1)S(1)}, bf16[2,256,128]{2,1,0:T(8,128)(2,1)S(1)}, u32[]{:S(2)}, u32[]{:S(2)}) collective-permute-start(bf16[2,256,128]{2,1,0:T(8,128)(2,1)S(1)} %fusion), channel_id=1, source_target_pairs={{0,2},{2,0},{1,3},{3,1},{4,6},{6,4},{5,7},{7,5},{8,10},{10,8},{9,1... | collective-permute-start | bytes 393224 | tf_op jit(solution)/shard_map/ppermute | solution.py:334
  29.5 6.8 %collective-permute-start.4 = (bf16[2,128,128]{2,1,0:T(8,128)(2,1)S(1)}, bf16[2,128,128]{2,1,0:T(8,128)(2,1)S(1)}, u32[]{:S(2)}, u32[]{:S(2)}) collective-permute-start(bf16[2,128,128]{2,1,0:T(8,128)(2,1)S(1)} %get-tuple-element.19), channel_id=1, source_target_pairs={{0,4},{4,8},{8,12},{12,0},{1,5},{5,9},{9,13},{13,1},{2,6},{6,10},{... | collective-permute-start | bytes 196616 | tf_op jit(solution)/shard_map/ppermute | solution.py:334
  31.2 7.2 %collective-permute-start.5 = (bf16[2,128,128]{2,1,0:T(8,128)(2,1)S(1)}, bf16[2,128,128]{2,1,0:T(8,128)(2,1)S(1)}, u32[]{:S(2)}, u32[]{:S(2)}) collective-permute-start(bf16[2,128,128]{2,1,0:T(8,128)(2,1)S(1)} %get-tuple-element.18), channel_id=1, source_target_pairs={{0,8},{4,12},{8,0},{12,4},{1,9},{5,13},{9,1},{13,5},{2,10},{6,14},... | collective-permute-start | bytes 196616 | tf_op jit(solution)/shard_map/ppermute | solution.py:334
  33.7 4.7 %collective-permute-start.6 = (bf16[2,128,128]{2,1,0:T(8,128)(2,1)S(1)}, bf16[2,128,128]{2,1,0:T(8,128)(2,1)S(1)}, u32[]{:S(2)}, u32[]{:S(2)}) collective-permute-start(bf16[2,128,128]{2,1,0:T(8,128)(2,1)S(1)} %get-tuple-element.17), channel_id=1, source_target_pairs={{0,12},{4,0},{8,4},{12,8},{1,13},{5,1},{9,5},{13,9},{2,14},{6,2},{... | collective-permute-start | bytes 196616 | tf_op jit(solution)/shard_map/ppermute | solution.py:334

commit v3 on v2

--- a/solution.py
+++ b/solution.py
@@ -199,8 +199,8 @@
     return d, base + jnp.where(d < extra, 1, 0), d * base + jnp.minimum(d, extra)
 
 
-def first_levels(dims, om_h, src, rcv, slow_h, T_h, K2_h, win_h, st, own_out,
-                 om, raw, slow, T, K2, win, P, c, D, sem_in, sem_t):
+def first_levels(dims, om_h, src, rcv, slow_h, T_h, K2_h, win_h, st, own_out, slow, T, K2, win, om_out,
+                 om, raw, P, c, D, sem_in, sem_t):
     n, slots, L, fronts, depth = dims
     d, nf, f0 = share(fronts, depth)
 
@@ -227,6 +227,8 @@
             prep(n, raw.at[j, f], st.at[j, f])
     for m in tables:
         m.wait()
+    for f in range(fronts):
+        om_out[0, f] = om[0, f]
 
     def level(z, _):
         s0 = level_prep(n, slow.at[z], win, D)
@@ -350,18 +352,18 @@
     got = jnp.stack([shift(sent, "depth", r) for r in range(1, depth)])
 
     math_scratch = [V((2, h + 8, n), F32), V((2, n, n), F32), V((2, n, n), F32)]
-    state, own_a = pl.pallas_call(
+    state, own_a, slow_v, T_v, K2_v, win_v, om = pl.pallas_call(
         functools.partial(first_levels, (n, slots, L, fronts, depth)),
-        out_shape=(S((slots, 2, 2, n, n), BF16), S((L, n, n), F32)),
+        out_shape=(S((slots, 2, 2, n, n), BF16), S((L, n, n), F32), S((L, n, n), F32), S((4, 2, n, n), BF16),
+                   S((h + 8, h), F32), S((n, n), F32), S((1, fronts), F32)),
         in_specs=[HBM] * 7,
-        out_specs=(VM, VM),
-        scratch_shapes=[pltpu.SMEM((1, fronts), F32), V((slots, 2, 2, n, n), F32), V((L, n, n), F32),
-                        V((4, 2, n, n), BF16), V((h + 8, h), F32), V((n, n), F32)] + math_scratch
+        out_specs=(VM, VM, VM, VM, VM, VM, SM),
+        scratch_shapes=[pltpu.SMEM((1, fronts), F32), V((slots, 2, 2, n, n), F32)] + math_scratch
         + [pltpu.SemaphoreType.DMA((slots, 2)), pltpu.SemaphoreType.DMA((5,))],
-        compiler_params=params(50),
+        compiler_params=params(40),
         cost_estimate=pl.CostEstimate(flops=8 * 10**9, bytes_accessed=10**7, transcendentals=10**6),
         name="first_levels",
-    )(omegas, source[0], receiver[0], slow, T, K2, win)
+    )(*[pltpu.with_memory_space_constraint(a, pltpu.HBM) for a in (omegas, source[0], receiver[0], slow, jnp.asarray(T), jnp.asarray(K2), jnp.asarray(win))])
 
     keep_own, send_own, keep_oth, send_oth, _ = pl.pallas_call(
         functools.partial(other_levels, (n, L, fronts, depth, freq)),
@@ -375,7 +377,7 @@
         compiler_params=params(32),
         cost_estimate=pl.CostEstimate(flops=8 * 10**9, bytes_accessed=10**7, transcendentals=10**6),
         name="other_levels",
-    )(omegas, state, slow, got, own_a, T, K2, win)
+    )(om, state, slow_v, got, own_a, T_v, K2_v, win_v)
 
     own, oth = keep_own, keep_oth
     for r in range(1, freq):

time: 39.5 us -> 35.5 us (0.90)
  local copies, waits for them, and re-layouts: 4.77 us -> 0.02 us
  Pallas kernels: 14.3 us -> 15.2 us
    unnamed x10 -> x0, local copies, waits for them, and re-layouts: 4.75 us -> none
    pallas_call x1, Pallas kernels: 7.23 us -> 8.22 us  [local(): pl.pallas_call(functools.partial(first_levels, (n, slots, L, fronts, dept...]
  transfers between devices with their start and end apart: 7 -> 7, of which waited for: 6 -> 6; matrix products, arithmetic and copies ran while one was open for 0% -> 0% of each run, Pallas kernels for 18% -> 23%
where the time goes in v3:
time: 35.5 us; the launch traced here: 35.4 us
  Pallas kernels  15.2 us (43%)
  starting transfers between devices  9.66 us (27%)
  waiting for transfers between devices  8.59 us (24%)
  other arithmetic  1.14 us (3%)
  between operations  0.71 us (2%)
    ppermute x7, starting transfers between devices, shift(): lax.ppermute(array, axis, [(i, (i + by) % size) for i in range(size)])  9.66 us
    ppermute x7, waiting for transfers between devices, shift(): lax.ppermute(array, axis, [(i, (i + by) % size) for i in range(size)])  8.59 us
    pallas_call x1, Pallas kernels, local(): pl.pallas_call(functools.partial(first_levels, (n, slots, L, fronts, dept...  8.22 us
    pallas_call x1, Pallas kernels, local(): pl.pallas_call(functools.partial(other_levels, (n, L, fronts, depth, freq...  6.16 us
    convert_element_type x1, other arithmetic, local(): sent = (slow - 1.0).astype(BF16)  1.08 us
    pallas_call x1, Pallas kernels, local(): pl.pallas_call(functools.partial(gather, (L, shots)), out_shape=S((TILE,...  0.75 us
  transfers between devices with their start and end apart: 7, of which 6 were waited for; matrix products, arithmetic and copies ran while one was open for 0% of the time, Pallas kernels for 23%

profile of v3, /device:TPU:0, one launch (start us, length us, event | category | flops | bytes accessed | tf_op | source)
XLA Modules:
  0.0 35.4 jit_solution(18373651856076227993)
XLA Ops:
  0.0 1.1 %add_convert_fusion = bf16[2,256,256]{2,1,0:T(8,128)(2,1)S(1)} fusion(f32[1,2,256,256]{3,2,1,0:T(8,128)} %param.10), kind=kLoop, calls=%fused_computation | loop fusion | flops 262144 | bytes 786432 | tf_op jit(solution)/shard_map/convert_element_type | solution.py:351
  1.1 3.0 %collective-permute-start = (bf16[2,256,256]{2,1,0:T(8,128)(2,1)S(1)}, bf16[2,256,256]{2,1,0:T(8,128)(2,1)S(1)}, u32[]{:S(2)}, u32[]{:S(2)}) collective-permute-start(bf16[2,256,256]{2,1,0:T(8,128)(2,1)S(1)} %add_convert_fusion), channel_id=1, source_target_pairs={{0,2},{2,0},{1,3},{3,1},{4,6},{6,4},{5,7},{7,5},{8,10},{10,8},{9,1... | collective-permute-start | bytes 786440 | tf_op jit(solution)/shard_map/ppermute | solution.py:336
  4.1 8.2 %first_levels.1 = (bf16[2,2,2,256,256]{4,3,2,1,0:T(8,128)(2,1)S(1)}, f32[2,256,256]{2,1,0:T(8,128)S(1)}, f32[2,256,256]{2,1,0:T(8,128)S(1)}, bf16[4,2,256,256]{3...) custom-call(f32[1,3]{1,0:T(1,128)} %om_h.1, ...), custom_call_target="tpu_custom_call" | custom-call | flops 8000000000 | bytes 10000000 | tf_op jit(solution)/shard_map/first_levels/pallas_call | solution.py:355
  12.3 0.0 collective-permute-done
  12.4 6.2 %other_levels.1 = (f32[2,256,128]{2,1,0:T(8,128)S(1)}, bf16[1,2,256,128]{3,2,1,0:T(8,128)(2,1)S(1)}, f32[1,2,256,128]{3,2,1,0:T(8,128)S(1)}, bf16[1,1,2,256,128]...) custom-call(f32[1,3]{1,0:T(1,128)S(1)} %get-tuple-element.16.om, ...), custom_call_target="tpu_custom_call", output_to_operand_aliasing={{4}: (1, {})} | custom-call | flops 8000000000 | bytes 10000000 | tf_op jit(solution)/shard_map/other_levels/pallas_call | solution.py:368
  18.5 0.1 collective-permute-start.2
  19.3 0.6 %collective-permute-start.1 = (bf16[2,256,128]{2,1,0:T(8,128)(2,1)S(1)}, bf16[2,256,128]{2,1,0:T(8,128)(2,1)S(1)}, u32[]{:S(2)}, u32[]{:S(2)}) collective-permute-start(bf16[2,256,128]{2,1,0:T(8,128)(2,1)S(1)} %bitcast.20), channel_id=1, source_target_pairs={{0,1},{1,0},{2,3},{3,2},{4,5},{5,4},{6,7},{7,6},{8,9},{9,8},{10,11... | collective-permute-start | bytes 393224 | tf_op jit(solution)/shard_map/ppermute | solution.py:336
  19.8 0.1 collective-permute-done.2
  20.0 0.4 %collective-permute-start.3 = (bf16[2,256,128]{2,1,0:T(8,128)(2,1)S(1)}, bf16[2,256,128]{2,1,0:T(8,128)(2,1)S(1)}, u32[]{:S(2)}, u32[]{:S(2)}) collective-permute-start(bf16[2,256,128]{2,1,0:T(8,128)(2,1)S(1)} %fusion), channel_id=1, source_target_pairs={{0,2},{2,0},{1,3},{3,1},{4,6},{6,4},{5,7},{7,5},{8,10},{10,8},{9,1... | collective-permute-start | bytes 393224 | tf_op jit(solution)/shard_map/ppermute | solution.py:336
  20.4 0.4 %collective-permute-done.1 = bf16[2,256,128]{2,1,0:T(8,128)(2,1)S(1)} collective-permute-done((bf16[2,256,128]{2,1,0:T(8,128)(2,1)S(1)}, bf16[2,256,128]{2,1,0:T(8,128)(2,1)S(1)}, u32[]{:S(2)}, u32[]{:S(2)}) %collective-permute-start.1) | collective-permute-done | bytes 131104 | tf_op jit(solution)/shard_map/ppermute | solution.py:336
  20.8 4.8 %collective-permute-done.3 = bf16[2,256,128]{2,1,0:T(8,128)(2,1)S(1)} collective-permute-done((bf16[2,256,128]{2,1,0:T(8,128)(2,1)S(1)}, bf16[2,256,128]{2,1,0:T(8,128)(2,1)S(1)}, u32[]{:S(2)}, u32[]{:S(2)}) %collective-permute-start.3) | collective-permute-done | bytes 131104 | tf_op jit(solution)/shard_map/ppermute | solution.py:336
  25.6 0.1 place.1
  25.7 1.6 %collective-permute-start.4 = (bf16[2,128,128]{2,1,0:T(8,128)(2,1)S(1)}, bf16[2,128,128]{2,1,0:T(8,128)(2,1)S(1)}, u32[]{:S(2)}, u32[]{:S(2)}) collective-permute-start(bf16[2,128,128]{2,1,0:T(8,128)(2,1)S(1)} %get-tuple-element.29), channel_id=1, source_target_pairs={{0,4},{4,8},{8,12},{12,0},{1,5},{5,9},{9,13},{13,1},{2,6},{6,10},{... | collective-permute-start | bytes 196616 | tf_op jit(solution)/shard_map/ppermute | solution.py:336
  27.4 2.6 %collective-permute-start.5 = (bf16[2,128,128]{2,1,0:T(8,128)(2,1)S(1)}, bf16[2,128,128]{2,1,0:T(8,128)(2,1)S(1)}, u32[]{:S(2)}, u32[]{:S(2)}) collective-permute-start(bf16[2,128,128]{2,1,0:T(8,128)(2,1)S(1)} %get-tuple-element.28), channel_id=1, source_target_pairs={{0,8},{4,12},{8,0},{12,4},{1,9},{5,13},{9,1},{13,5},{2,10},{6,14},... | collective-permute-start | bytes 196616 | tf_op jit(solution)/shard_map/ppermute | solution.py:336
  30.0 1.3 %collective-permute-start.6 = (bf16[2,128,128]{2,1,0:T(8,128)(2,1)S(1)}, bf16[2,128,128]{2,1,0:T(8,128)(2,1)S(1)}, u32[]{:S(2)}, u32[]{:S(2)}) collective-permute-start(bf16[2,128,128]{2,1,0:T(8,128)(2,1)S(1)} %get-tuple-element.27), channel_id=1, source_target_pairs={{0,12},{4,0},{8,4},{12,8},{1,13},{5,1},{9,5},{13,9},{2,14},{6,2},{... | collective-permute-start | bytes 196616 | tf_op jit(solution)/shard_map/ppermute | solution.py:336
  31.3 1.3 %collective-permute-done.4.refs_1_ = bf16[2,128,128]{2,1,0:T(8,128)(2,1)S(1)} collective-permute-done((bf16[2,128,128]{2,1,0:T(8,128)(2,1)S(1)}, bf16[2,128,128]{2,1,0:T(8,128)(2,1)S(1)}, u32[]{:S(2)}, u32[]{:S(2)}) %collective-permute-start.4) | collective-permute-done | bytes 65568 | tf_op jit(solution)/shard_map/ppermute | solution.py:336
  32.6 2.0 %collective-permute-done.5.refs_2_ = bf16[2,128,128]{2,1,0:T(8,128)(2,1)S(1)} collective-permute-done((bf16[2,128,128]{2,1,0:T(8,128)(2,1)S(1)}, bf16[2,128,128]{2,1,0:T(8,128)(2,1)S(1)}, u32[]{:S(2)}, u32[]{:S(2)}) %collective-permute-start.5) | collective-permute-done | bytes 65568 | tf_op jit(solution)/shard_map/ppermute | solution.py:336
  34.6 0.1 collective-permute-done.6.refs_3_
  34.6 0.7 %gather.1 = f32[128,2,128]{2,1,0:T(2,128)} custom-call(bf16[2,128,128]{2,1,0:T(8,128)(2,1)S(1)} %get-tuple-element.30.refs_0_, bf16[2,128,128]{2,1,0:T(8,128)(2,1)S(1)} %collective-permute-done.4.refs_1_, bf16[2,128,128]{2,1,0:T(8,128)(2,1)S(1)} %collective-permute-done.5.refs_2_, bf16[2,128,128]{2,1,0:T(8,128)(2,1)S(1)} %collective-permute-done.6.refs_3_), custom_call_target="tpu_custom_call" | custom-call | tf_op jit(solution)/shard_map/gather/pallas_call | solution.py:400
  (3 shorter events, 0.1 us)
Async XLA Ops:
  1.1 11.3 %collective-permute-start = (bf16[2,256,256]{2,1,0:T(8,128)(2,1)S(1)}, bf16[2,256,256]{2,1,0:T(8,128)(2,1)S(1)}, u32[]{:S(2)}, u32[]{:S(2)}) collective-permute-start(bf16[2,256,256]{2,1,0:T(8,128)(2,1)S(1)} %add_convert_fusion), channel_id=1, source_target_pairs={{0,2},{2,0},{1,3},{3,1},{4,6},{6,4},{5,7},{7,5},{8,10},{10,8},{9,1... | collective-permute-start | bytes 786440 | tf_op jit(solution)/shard_map/ppermute | solution.py:336
  18.5 1.4 %collective-permute-start.2 = (bf16[1,2,256,128]{3,2,1,0:T(8,128)(2,1)S(1)}, bf16[1,2,256,128]{3,2,1,0:T(8,128)(2,1)S(1)}, u32[]{:S(2)}, u32[]{:S(2)}) collective-permute-start(bf16[1,2,256,128]{3,2,1,0:T(8,128)(2,1)S(1)} %bitcast.21), channel_id=1, source_target_pairs={{0,1},{1,0},{2,3},{3,2},{4,5},{5,4},{6,7},{7,6},{8,9},{9,8},{10,11... | collective-permute-start | bytes 393224 | tf_op jit(solution)/shard_map/ppermute | solution.py:336
  19.3 1.6 %collective-permute-start.1 = (bf16[2,256,128]{2,1,0:T(8,128)(2,1)S(1)}, bf16[2,256,128]{2,1,0:T(8,128)(2,1)S(1)}, u32[]{:S(2)}, u32[]{:S(2)}) collective-permute-start(bf16[2,256,128]{2,1,0:T(8,128)(2,1)S(1)} %bitcast.20), channel_id=1, source_target_pairs={{0,1},{1,0},{2,3},{3,2},{4,5},{5,4},{6,7},{7,6},{8,9},{9,8},{10,11... | collective-permute-start | bytes 393224 | tf_op jit(solution)/shard_map/ppermute | solution.py:336
  20.0 5.6 %collective-permute-start.3 = (bf16[2,256,128]{2,1,0:T(8,128)(2,1)S(1)}, bf16[2,256,128]{2,1,0:T(8,128)(2,1)S(1)}, u32[]{:S(2)}, u32[]{:S(2)}) collective-permute-start(bf16[2,256,128]{2,1,0:T(8,128)(2,1)S(1)} %fusion), channel_id=1, source_target_pairs={{0,2},{2,0},{1,3},{3,1},{4,6},{6,4},{5,7},{7,5},{8,10},{10,8},{9,1... | collective-permute-start | bytes 393224 | tf_op jit(solution)/shard_map/ppermute | solution.py:336
  25.7 6.8 %collective-permute-start.4 = (bf16[2,128,128]{2,1,0:T(8,128)(2,1)S(1)}, bf16[2,128,128]{2,1,0:T(8,128)(2,1)S(1)}, u32[]{:S(2)}, u32[]{:S(2)}) collective-permute-start(bf16[2,128,128]{2,1,0:T(8,128)(2,1)S(1)} %get-tuple-element.29), channel_id=1, source_target_pairs={{0,4},{4,8},{8,12},{12,0},{1,5},{5,9},{9,13},{13,1},{2,6},{6,10},{... | collective-permute-start | bytes 196616 | tf_op jit(solution)/shard_map/ppermute | solution.py:336
  27.4 7.2 %collective-permute-start.5 = (bf16[2,128,128]{2,1,0:T(8,128)(2,1)S(1)}, bf16[2,128,128]{2,1,0:T(8,128)(2,1)S(1)}, u32[]{:S(2)}, u32[]{:S(2)}) collective-permute-start(bf16[2,128,128]{2,1,0:T(8,128)(2,1)S(1)} %get-tuple-element.28), channel_id=1, source_target_pairs={{0,8},{4,12},{8,0},{12,4},{1,9},{5,13},{9,1},{13,5},{2,10},{6,14},... | collective-permute-start | bytes 196616 | tf_op jit(solution)/shard_map/ppermute | solution.py:336
  30.0 4.7 %collective-permute-start.6 = (bf16[2,128,128]{2,1,0:T(8,128)(2,1)S(1)}, bf16[2,128,128]{2,1,0:T(8,128)(2,1)S(1)}, u32[]{:S(2)}, u32[]{:S(2)}) collective-permute-start(bf16[2,128,128]{2,1,0:T(8,128)(2,1)S(1)} %get-tuple-element.27), channel_id=1, source_target_pairs={{0,12},{4,0},{8,4},{12,8},{1,13},{5,1},{9,5},{13,9},{2,14},{6,2},{... | collective-permute-start | bytes 196616 | tf_op jit(solution)/shard_map/ppermute | solution.py:336

commit v4 on v3

--- a/solution.py
+++ b/solution.py
@@ -19,7 +19,7 @@
 def _cosr(a): return np.cos(np.sqrt(a))
 def _sinr(a): return np.sinc(np.sqrt(a) / np.pi)
 PC = _fit(_cosr, 12.5, 6); PS = _fit(_sinr, 12.5, 5)
-CC = _fit(_cosr, 4.1, 5); CS = _fit(_sinr, 4.1, 4)
+CC = _fit(lambda a: (_cosr(a) - 1) / a, 4.1, 4); CS = _fit(_sinr, 4.1, 4)
 
 def horner(co, x):
     r = co[-1] * x + co[-2]
@@ -64,8 +64,10 @@
 def level_prep(n, s, win, D):
     s0 = jnp.sum(s[...]) * (1.0 / (n * n))
     d = s[...] - s0
-    D[0] = d * d
+    x = d * d
+    D[0] = x
     D[1] = d * win[...]
+    D[2] = x * win[...]
     return s0
 
 def propagator(n, w2, K2, P):
@@ -105,18 +107,18 @@
     o = P[comp, g + 8:h + 8]
     return jnp.concatenate([o, o], axis=0)
 
-def corr(n, om, win, D, c):
-    o2 = om * om
-    cc, cs, f = [], [], jnp.float32(1.0)
-    for k in range(max(len(CC), len(CS))):
-        if k < len(CC): cc.append(CC[k] * f)
-        if k < len(CS): cs.append(CS[k] * f * om)
-        f = f * o2
+def corr(om, win, D, c):
+    cc, cs, f = [], [], om
+    for k in range(len(CC)):
+        cs.append(CS[k] * f)
+        f = f * om
+        cc.append(CC[k] * f)
+        f = f * om
     x = D[0]
-    c[0] = win[...] * horner(cc, x)
+    c[0] = win[...] + D[2] * horner(cc, x)
     c[1] = D[1] * horner(cs, x)
 
-def front_math(n, om, s0, T, K2, win, st, part, P, c, D):
+def front_math(n, om, s0, T, K2, win, st, P, c, D):
     h = n // 2
     f32, bf = jnp.float32, jnp.bfloat16
     dot = functools.partial(jnp.dot, preferred_element_type=f32)
@@ -144,7 +146,7 @@
             else:
                 out.append(jnp.concatenate([wr * pr + wi * pi, wi * pr - wr * pi], axis=0).astype(bf))
         W2.append(out)
-    corr(n, om, win, D, c)
+    corr(om, win, D, c)
     YY = []
     for f, sg in FL:
         E = dot(T[2, 0], W2[f][0]); O = dot(T[2, 1], W2[f][1])
@@ -171,10 +173,20 @@
         st[f, 0] = jnp.concatenate([r0 + r1, i0 + i1], axis=1).astype(bf)
         st[f, 1] = jnp.concatenate([r0 - r1, i0 - i1], axis=1).astype(bf)
         res.append(halves)
+    terms = []
     for hf in (0, 1):
         (ur, ui), (wr, wi) = res[0][hf], res[1][hf]
-        sl = slice(hf * h, (hf + 1) * h)
-        part[:, sl] = part[:, sl] + (ur * wr + ui * wi)
+        terms.append(ur * wr + ui * wi)
+    return terms
+
+
+def level_math(n, oms, s, T, K2, win, st, part, P, c, D):
+    h = n // 2
+    s0 = level_prep(n, s, win, D)
+    terms = [front_math(n, om, s0, T, K2, win, st.at[j], P.at[j], c.at[j], D) for j, om in enumerate(oms)]
+    for hf in (0, 1):
+        part[:, hf * h:(hf + 1) * h] = functools.reduce(lambda a, b: a + b, [t[hf] for t in terms])
+
 
 def prep(n, src, st_ab):
     h = n // 2
@@ -199,7 +211,7 @@
     return d, base + jnp.where(d < extra, 1, 0), d * base + jnp.minimum(d, extra)
 
 
-def first_levels(dims, om_h, src, rcv, slow_h, T_h, K2_h, win_h, st, own_out, slow, T, K2, win, om_out,
+def first_levels(dims, om_h, slow_h, T_h, K2_h, win_h, src, rcv, st, own_out, slow, T, K2, win, om_out,
                  om, raw, P, c, D, sem_in, sem_t):
     n, slots, L, fronts, depth = dims
     d, nf, f0 = share(fronts, depth)
@@ -211,34 +223,40 @@
             pltpu.make_async_copy(rcv.at[fr], raw.at[j, 1], sem_in.at[j, 1]),
         )
 
-    tables = [
+    small = [
         pltpu.make_async_copy(a, b, sem_t.at[i])
         for i, (a, b) in enumerate(((om_h, om), (slow_h, slow), (T_h, T), (K2_h, K2), (win_h, win)))
     ]
-    for j in range(slots):
+
+    def each(j, act):
+        if j < fronts // depth:
+            act()
+        else:
+            pl.when(j < nf)(act)
+
+    def begin(j):
         for m in moves(j):
             m.start()
-        if j == 0:
-            for m in tables:
-                m.start()
-    for j in range(slots):
+
+    def ready(j):
         for f, m in enumerate(moves(j)):
             m.wait()
             prep(n, raw.at[j, f], st.at[j, f])
-    for m in tables:
+
+    each(0, lambda: begin(0))
+    for m in small:
+        m.start()
+    for j in range(1, slots):
+        each(j, functools.partial(begin, j))
+    for j in range(slots):
+        each(j, functools.partial(ready, j))
+    for m in small:
         m.wait()
     for f in range(fronts):
         om_out[0, f] = om[0, f]
 
     def level(z, _):
-        s0 = level_prep(n, slow.at[z], win, D)
-        own_out[z] = jnp.zeros((n, n), F32)
-
-        def front(j, _):
-            front_math(n, om[0, f0 + j], s0, T, K2, win, st.at[j], own_out.at[z], P, c, D)
-            return 0
-
-        lax.fori_loop(0, nf, front, 0)
+        level_math(n, [om[0, f0 + j] for j in range(slots)], slow.at[z], T, K2, win, st, own_out.at[z], P, c, D)
         return 0
 
     lax.fori_loop(0, jnp.where(d == 0, L, 0), level, 0)
@@ -246,7 +264,7 @@
 
 def other_levels(dims, om, st_in, slow, got, own_in, T, K2, win, keep_own, send_own, keep_oth, send_oth, st,
                  s_now, part, P, c, D):
-    n, L, fronts, depth, freq = dims
+    n, slots, L, fronts, depth, freq = dims
     d, nf, f0 = share(fronts, depth)
     fq = lax.axis_index("freq")
     lo = jnp.where(d == 0, L, 0)
@@ -279,14 +297,15 @@
         def _():
             s_now[...] = got[jnp.maximum(back - 1, 0), zl].astype(F32) + 1.0
 
-        s0 = level_prep(n, s_now, win, D)
-        part[...] = jnp.zeros((n, n), F32)
-
-        def front(j, _):
-            front_math(n, om[0, f0 + j], s0, T, K2, win, st.at[j], part, P, c, D)
-            return 0
-
-        lax.fori_loop(0, nf, front, 0)
+        for count in sorted({slots, fronts // depth} - {0}):
+            @pl.when(nf == count)
+            def _():
+                level_math(n, [om[0, f0 + j] for j in range(count)], s_now, T, K2, win, st, part, P, c, D)
+
+        if fronts < depth:
+            @pl.when(nf == 0)
+            def _():
+                part[...] = jnp.zeros((n, n), F32)
 
         @pl.when(back == 0)
         def _():
@@ -331,6 +350,10 @@
         out[:, z, :] = total
 
 
+def pinned(array):
+    return pltpu.with_memory_space_constraint(array, pltpu.HBM)
+
+
 def shift(array, axis, by):
     size = lax.axis_size(axis)
     return lax.ppermute(array, axis, [(i, (i + by) % size) for i in range(size)])
@@ -351,7 +374,7 @@
     sent = (slow - 1.0).astype(BF16)
     got = jnp.stack([shift(sent, "depth", r) for r in range(1, depth)])
 
-    math_scratch = [V((2, h + 8, n), F32), V((2, n, n), F32), V((2, n, n), F32)]
+    math_scratch = [V((slots, 2, h + 8, n), F32), V((slots, 2, n, n), F32), V((3, n, n), F32)]
     state, own_a, slow_v, T_v, K2_v, win_v, om = pl.pallas_call(
         functools.partial(first_levels, (n, slots, L, fronts, depth)),
         out_shape=(S((slots, 2, 2, n, n), BF16), S((L, n, n), F32), S((L, n, n), F32), S((4, 2, n, n), BF16),
@@ -363,10 +386,10 @@
         compiler_params=params(40),
         cost_estimate=pl.CostEstimate(flops=8 * 10**9, bytes_accessed=10**7, transcendentals=10**6),
         name="first_levels",
-    )(*[pltpu.with_memory_space_constraint(a, pltpu.HBM) for a in (omegas, source[0], receiver[0], slow, jnp.asarray(T), jnp.asarray(K2), jnp.asarray(win))])
+    )(*map(pinned, (omegas, slow, jnp.asarray(T), jnp.asarray(K2), jnp.asarray(win), source[0], receiver[0])))
 
     keep_own, send_own, keep_oth, send_oth, _ = pl.pallas_call(
-        functools.partial(other_levels, (n, L, fronts, depth, freq)),
+        functools.partial(other_levels, (n, slots, L, fronts, depth, freq)),
         out_shape=(S((L, n, w), F32), S((freq - 1, L, n, w), BF16),
                    S((depth - 1, L, n, w), F32), S((freq - 1, depth - 1, L, n, w), BF16),
                    S(state.shape, state.dtype)),
@@ -385,6 +408,7 @@
     for r in range(1, freq):
         own = own + shift(send_own[r - 1], "freq", r).astype(F32)
     oth = oth.astype(BF16)
+    own, start = lax.optimization_barrier((own, shot_start))
     arrived = jnp.stack([shift(oth[r - 1], "depth", r) for r in range(1, depth)])
 
     blocks = pl.pallas_call(
@@ -395,7 +419,7 @@
         scratch_shapes=[V((L, 2 * shots * TILE + n, w), F32)],
         compiler_params=params(32),
         name="place",
-    )(shot_start, own, arrived)
+    )(start, own, arrived)
     pieces = [blocks[0]] + [shift(blocks[r], "shot", r) for r in range(1, shots)]
     return pl.pallas_call(
         functools.partial(gather, (L, shots)),

time: 35.5 us -> 33.4 us (0.941)
  Pallas kernels: 15.2 us -> 13.1 us
  starting transfers between devices: 9.66 us -> 10.7 us
  waiting for transfers between devices: 8.59 us -> 7.58 us
    pallas_call x1, Pallas kernels: 8.22 us -> 7.14 us  [local(): pl.pallas_call(functools.partial(first_levels, (n, slots, L, fronts, dept...]
    pallas_call x1, Pallas kernels: 6.16 us -> 5.1 us  [local(): pl.pallas_call(functools.partial(other_levels, (n, slots, L, fronts, dept...]
    ppermute x7, starting transfers between devices: 9.66 us -> 10.7 us  [shift(): lax.ppermute(array, axis, [(i, (i + by) % size) for i in range(size)])]
    ppermute x7, waiting for transfers between devices: 8.59 us -> 7.58 us  [shift(): lax.ppermute(array, axis, [(i, (i + by) % size) for i in range(size)])]
  transfers between devices with their start and end apart: 7 -> 7, of which waited for: 6 -> 5; matrix products, arithmetic and copies ran while one was open for 0% -> 0% of each run, Pallas kernels for 23% -> 22%
where the time goes in v4:
time: 33.4 us; the launch traced here: 33.2 us
  Pallas kernels  13.1 us (39%)
  starting transfers between devices  10.7 us (32%)
  waiting for transfers between devices  7.58 us (23%)
  other arithmetic  1.14 us (3%)
  between operations  0.71 us (2%)
    ppermute x7, starting transfers between devices, shift(): lax.ppermute(array, axis, [(i, (i + by) % size) for i in range(size)])  10.7 us
    ppermute x7, waiting for transfers between devices, shift(): lax.ppermute(array, axis, [(i, (i + by) % size) for i in range(size)])  7.58 us
    pallas_call x1, Pallas kernels, local(): pl.pallas_call(functools.partial(first_levels, (n, slots, L, fronts, dept...  7.14 us
    pallas_call x1, Pallas kernels, local(): pl.pallas_call(functools.partial(other_levels, (n, slots, L, fronts, dept...  5.1 us
    convert_element_type x1, other arithmetic, local(): sent = (slow - 1.0).astype(BF16)  1.08 us
    pallas_call x1, Pallas kernels, local(): pl.pallas_call(functools.partial(gather, (L, shots)), out_shape=S((TILE,...  0.75 us
  transfers between devices with their start and end apart: 7, of which 5 were waited for; matrix products, arithmetic and copies ran while one was open for 0% of the time, Pallas kernels for 22%

profile of v4, /device:TPU:0, one launch (start us, length us, event | category | flops | bytes accessed | tf_op | source)
XLA Modules:
  0.0 33.2 jit_solution(9974034240581872593)
XLA Ops:
  0.0 1.1 %add_convert_fusion = bf16[2,256,256]{2,1,0:T(8,128)(2,1)S(1)} fusion(f32[1,2,256,256]{3,2,1,0:T(8,128)} %param.10), kind=kLoop, calls=%fused_computation | loop fusion | flops 262144 | bytes 786432 | tf_op jit(solution)/shard_map/convert_element_type | solution.py:374
  1.1 3.0 %collective-permute-start = (bf16[2,256,256]{2,1,0:T(8,128)(2,1)S(1)}, bf16[2,256,256]{2,1,0:T(8,128)(2,1)S(1)}, u32[]{:S(2)}, u32[]{:S(2)}) collective-permute-start(bf16[2,256,256]{2,1,0:T(8,128)(2,1)S(1)} %add_convert_fusion), channel_id=1, source_target_pairs={{0,2},{2,0},{1,3},{3,1},{4,6},{6,4},{5,7},{7,5},{8,10},{10,8},{9,1... | collective-permute-start | bytes 786440 | tf_op jit(solution)/shard_map/ppermute | solution.py:359
  4.1 7.1 %first_levels.1 = (bf16[2,2,2,256,256]{4,3,2,1,0:T(8,128)(2,1)S(1)}, f32[2,256,256]{2,1,0:T(8,128)S(1)}, f32[2,256,256]{2,1,0:T(8,128)S(1)}, bf16[4,2,256,256]{3...) custom-call(f32[1,3]{1,0:T(1,128)} %om_h.1, ...), custom_call_target="tpu_custom_call" | custom-call | flops 8000000000 | bytes 10000000 | tf_op jit(solution)/shard_map/first_levels/pallas_call | solution.py:378
  11.3 0.0 collective-permute-done
  11.3 5.1 %other_levels.1 = (f32[2,256,128]{2,1,0:T(8,128)S(1)}, bf16[1,2,256,128]{3,2,1,0:T(8,128)(2,1)S(1)}, f32[1,2,256,128]{3,2,1,0:T(8,128)S(1)}, bf16[1,1,2,256,128]...) custom-call(f32[1,3]{1,0:T(1,128)S(1)} %get-tuple-element.18.om, ...), custom_call_target="tpu_custom_call", output_to_operand_aliasing={{4}: (1, {})} | custom-call | flops 8000000000 | bytes 10000000 | tf_op jit(solution)/shard_map/other_levels/pallas_call | solution.py:391
  16.4 0.1 collective-permute-start.2
  17.1 0.6 %collective-permute-start.1 = (bf16[2,256,128]{2,1,0:T(8,128)(2,1)S(1)}, bf16[2,256,128]{2,1,0:T(8,128)(2,1)S(1)}, u32[]{:S(2)}, u32[]{:S(2)}) collective-permute-start(bf16[2,256,128]{2,1,0:T(8,128)(2,1)S(1)} %bitcast.20), channel_id=1, source_target_pairs={{0,1},{1,0},{2,3},{3,2},{4,5},{5,4},{6,7},{7,6},{8,9},{9,8},{10,11... | collective-permute-start | bytes 393224 | tf_op jit(solution)/shard_map/ppermute | solution.py:359
  17.7 0.1 collective-permute-done.2
  17.8 1.4 %collective-permute-start.3 = (bf16[2,256,128]{2,1,0:T(8,128)(2,1)S(1)}, bf16[2,256,128]{2,1,0:T(8,128)(2,1)S(1)}, u32[]{:S(2)}, u32[]{:S(2)}) collective-permute-start(bf16[2,256,128]{2,1,0:T(8,128)(2,1)S(1)} %fusion), channel_id=1, source_target_pairs={{0,2},{2,0},{1,3},{3,1},{4,6},{6,4},{5,7},{7,5},{8,10},{10,8},{9,1... | collective-permute-start | bytes 393224 | tf_op jit(solution)/shard_map/ppermute | solution.py:359
  19.3 0.0 collective-permute-done.1
  19.3 4.1 %collective-permute-done.3 = bf16[2,256,128]{2,1,0:T(8,128)(2,1)S(1)} collective-permute-done((bf16[2,256,128]{2,1,0:T(8,128)(2,1)S(1)}, bf16[2,256,128]{2,1,0:T(8,128)(2,1)S(1)}, u32[]{:S(2)}, u32[]{:S(2)}) %collective-permute-start.3) | collective-permute-done | bytes 131104 | tf_op jit(solution)/shard_map/ppermute | solution.py:359
  23.5 0.1 place.1
  23.6 1.6 %collective-permute-start.4 = (bf16[2,128,128]{2,1,0:T(8,128)(2,1)S(1)}, bf16[2,128,128]{2,1,0:T(8,128)(2,1)S(1)}, u32[]{:S(2)}, u32[]{:S(2)}) collective-permute-start(bf16[2,128,128]{2,1,0:T(8,128)(2,1)S(1)} %get-tuple-element.33), channel_id=1, source_target_pairs={{0,4},{4,8},{8,12},{12,0},{1,5},{5,9},{9,13},{13,1},{2,6},{6,10},{... | collective-permute-start | bytes 196616 | tf_op jit(solution)/shard_map/ppermute | solution.py:359
  25.2 2.6 %collective-permute-start.5 = (bf16[2,128,128]{2,1,0:T(8,128)(2,1)S(1)}, bf16[2,128,128]{2,1,0:T(8,128)(2,1)S(1)}, u32[]{:S(2)}, u32[]{:S(2)}) collective-permute-start(bf16[2,128,128]{2,1,0:T(8,128)(2,1)S(1)} %get-tuple-element.32), channel_id=1, source_target_pairs={{0,8},{4,12},{8,0},{12,4},{1,9},{5,13},{9,1},{13,5},{2,10},{6,14},... | collective-permute-start | bytes 196616 | tf_op jit(solution)/shard_map/ppermute | solution.py:359
  27.8 1.3 %collective-permute-start.6 = (bf16[2,128,128]{2,1,0:T(8,128)(2,1)S(1)}, bf16[2,128,128]{2,1,0:T(8,128)(2,1)S(1)}, u32[]{:S(2)}, u32[]{:S(2)}) collective-permute-start(bf16[2,128,128]{2,1,0:T(8,128)(2,1)S(1)} %get-tuple-element.31), channel_id=1, source_target_pairs={{0,12},{4,0},{8,4},{12,8},{1,13},{5,1},{9,5},{13,9},{2,14},{6,2},{... | collective-permute-start | bytes 196616 | tf_op jit(solution)/shard_map/ppermute | solution.py:359
  29.2 1.3 %collective-permute-done.4.refs_1_ = bf16[2,128,128]{2,1,0:T(8,128)(2,1)S(1)} collective-permute-done((bf16[2,128,128]{2,1,0:T(8,128)(2,1)S(1)}, bf16[2,128,128]{2,1,0:T(8,128)(2,1)S(1)}, u32[]{:S(2)}, u32[]{:S(2)}) %collective-permute-start.4) | collective-permute-done | bytes 65568 | tf_op jit(solution)/shard_map/ppermute | solution.py:359
  30.4 2.0 %collective-permute-done.5.refs_2_ = bf16[2,128,128]{2,1,0:T(8,128)(2,1)S(1)} collective-permute-done((bf16[2,128,128]{2,1,0:T(8,128)(2,1)S(1)}, bf16[2,128,128]{2,1,0:T(8,128)(2,1)S(1)}, u32[]{:S(2)}, u32[]{:S(2)}) %collective-permute-start.5) | collective-permute-done | bytes 65568 | tf_op jit(solution)/shard_map/ppermute | solution.py:359
  32.4 0.1 collective-permute-done.6.refs_3_
  32.5 0.7 %gather.1 = f32[128,2,128]{2,1,0:T(2,128)} custom-call(bf16[2,128,128]{2,1,0:T(8,128)(2,1)S(1)} %get-tuple-element.34.refs_0_, bf16[2,128,128]{2,1,0:T(8,128)(2,1)S(1)} %collective-permute-done.4.refs_1_, bf16[2,128,128]{2,1,0:T(8,128)(2,1)S(1)} %collective-permute-done.5.refs_2_, bf16[2,128,128]{2,1,0:T(8,128)(2,1)S(1)} %collective-permute-done.6.refs_3_), custom_call_target="tpu_custom_call" | custom-call | tf_op jit(solution)/shard_map/gather/pallas_call | solution.py:424
  (3 shorter events, 0.1 us)
Async XLA Ops:
  1.1 10.2 %collective-permute-start = (bf16[2,256,256]{2,1,0:T(8,128)(2,1)S(1)}, bf16[2,256,256]{2,1,0:T(8,128)(2,1)S(1)}, u32[]{:S(2)}, u32[]{:S(2)}) collective-permute-start(bf16[2,256,256]{2,1,0:T(8,128)(2,1)S(1)} %add_convert_fusion), channel_id=1, source_target_pairs={{0,2},{2,0},{1,3},{3,1},{4,6},{6,4},{5,7},{7,5},{8,10},{10,8},{9,1... | collective-permute-start | bytes 786440 | tf_op jit(solution)/shard_map/ppermute | solution.py:359
  16.4 1.4 %collective-permute-start.2 = (bf16[1,2,256,128]{3,2,1,0:T(8,128)(2,1)S(1)}, bf16[1,2,256,128]{3,2,1,0:T(8,128)(2,1)S(1)}, u32[]{:S(2)}, u32[]{:S(2)}) collective-permute-start(bf16[1,2,256,128]{3,2,1,0:T(8,128)(2,1)S(1)} %bitcast.21), channel_id=1, source_target_pairs={{0,1},{1,0},{2,3},{3,2},{4,5},{5,4},{6,7},{7,6},{8,9},{9,8},{10,11... | collective-permute-start | bytes 393224 | tf_op jit(solution)/shard_map/ppermute | solution.py:359
  17.1 2.2 %collective-permute-start.1 = (bf16[2,256,128]{2,1,0:T(8,128)(2,1)S(1)}, bf16[2,256,128]{2,1,0:T(8,128)(2,1)S(1)}, u32[]{:S(2)}, u32[]{:S(2)}) collective-permute-start(bf16[2,256,128]{2,1,0:T(8,128)(2,1)S(1)} %bitcast.20), channel_id=1, source_target_pairs={{0,1},{1,0},{2,3},{3,2},{4,5},{5,4},{6,7},{7,6},{8,9},{9,8},{10,11... | collective-permute-start | bytes 393224 | tf_op jit(solution)/shard_map/ppermute | solution.py:359
  17.8 5.6 %collective-permute-start.3 = (bf16[2,256,128]{2,1,0:T(8,128)(2,1)S(1)}, bf16[2,256,128]{2,1,0:T(8,128)(2,1)S(1)}, u32[]{:S(2)}, u32[]{:S(2)}) collective-permute-start(bf16[2,256,128]{2,1,0:T(8,128)(2,1)S(1)} %fusion), channel_id=1, source_target_pairs={{0,2},{2,0},{1,3},{3,1},{4,6},{6,4},{5,7},{7,5},{8,10},{10,8},{9,1... | collective-permute-start | bytes 393224 | tf_op jit(solution)/shard_map/ppermute | solution.py:359
  23.6 6.8 %collective-permute-start.4 = (bf16[2,128,128]{2,1,0:T(8,128)(2,1)S(1)}, bf16[2,128,128]{2,1,0:T(8,128)(2,1)S(1)}, u32[]{:S(2)}, u32[]{:S(2)}) collective-permute-start(bf16[2,128,128]{2,1,0:T(8,128)(2,1)S(1)} %get-tuple-element.33), channel_id=1, source_target_pairs={{0,4},{4,8},{8,12},{12,0},{1,5},{5,9},{9,13},{13,1},{2,6},{6,10},{... | collective-permute-start | bytes 196616 | tf_op jit(solution)/shard_map/ppermute | solution.py:359
  25.2 7.2 %collective-permute-start.5 = (bf16[2,128,128]{2,1,0:T(8,128)(2,1)S(1)}, bf16[2,128,128]{2,1,0:T(8,128)(2,1)S(1)}, u32[]{:S(2)}, u32[]{:S(2)}) collective-permute-start(bf16[2,128,128]{2,1,0:T(8,128)(2,1)S(1)} %get-tuple-element.32), channel_id=1, source_target_pairs={{0,8},{4,12},{8,0},{12,4},{1,9},{5,13},{9,1},{13,5},{2,10},{6,14},... | collective-permute-start | bytes 196616 | tf_op jit(solution)/shard_map/ppermute | solution.py:359
  27.8 4.7 %collective-permute-start.6 = (bf16[2,128,128]{2,1,0:T(8,128)(2,1)S(1)}, bf16[2,128,128]{2,1,0:T(8,128)(2,1)S(1)}, u32[]{:S(2)}, u32[]{:S(2)}) collective-permute-start(bf16[2,128,128]{2,1,0:T(8,128)(2,1)S(1)} %get-tuple-element.31), channel_id=1, source_target_pairs={{0,12},{4,0},{8,4},{12,8},{1,13},{5,1},{9,5},{13,9},{2,14},{6,2},{... | collective-permute-start | bytes 196616 | tf_op jit(solution)/shard_map/ppermute | solution.py:359

commit v5 on v4

--- a/solution.py
+++ b/solution.py
@@ -205,16 +205,107 @@
     return pltpu.CompilerParams(vmem_limit_bytes=mib * 1024 * 1024)
 
 
-def share(fronts, depth):
-    d = lax.axis_index("depth")
-    base, extra = fronts // depth, fronts % depth
-    return d, base + jnp.where(d < extra, 1, 0), d * base + jnp.minimum(d, extra)
-
-
-def first_levels(dims, om_h, slow_h, T_h, K2_h, win_h, src, rcv, st, own_out, slow, T, K2, win, om_out,
-                 om, raw, P, c, D, sem_in, sem_t):
-    n, slots, L, fronts, depth = dims
-    d, nf, f0 = share(fronts, depth)
+class Plan:
+    def __init__(self, n, L, fronts, depth, freq):
+        self.n, self.L, self.fronts, self.depth, self.freq = n, L, fronts, depth, freq
+        self.levels = depth * L
+        self.base, self.extra = fronts // depth, fronts % depth
+        self.slots = self.base + (1 if self.extra else 0)
+
+    def share(self):
+        d = lax.axis_index("depth")
+        late = jnp.maximum(d - (self.depth - self.extra), 0)
+        more = jnp.where(d >= self.depth - self.extra, 1, 0)
+        return d, self.base + more, d * self.base + late
+
+    def span(self, step, d):
+        L, S = self.L, self.levels
+        first, last = d == 0, d == self.depth - 1
+        if step == 0:
+            return 0, jnp.where(first, L, 0)
+        if step == 1:
+            return jnp.where(first, L, 0), jnp.where(first, L + 1, 1)
+        if step == 2:
+            return jnp.where(first, L + 1, 1), jnp.where(last, S - L, S)
+        if step == 3:
+            return S - L, jnp.where(last, S - 1, S - L)
+        return S - 1, jnp.where(last, S, S - 1)
+
+    def counts(self, step):
+        of = [self.base + (1 if d >= self.depth - self.extra else 0) for d in range(self.depth)]
+        of = of[:1] if step == 0 else of[-1:] if step >= 3 else of
+        return sorted(set(of))
+
+
+def run_levels(plan, step, om, slow, got, T, K2, win, st, keep_own, send_own, keep_oth, send_oth, s_now, part, P, c, D):
+    n, L, depth, freq = plan.n, plan.L, plan.depth, plan.freq
+    d, nf, f0 = plan.share()
+    fq = lax.axis_index("freq")
+    w = n // freq
+
+    def split(keep, sends):
+        for a in range(freq):
+            @pl.when(fq == a)
+            def _():
+                keep[...] = part[:, a * w:(a + 1) * w]
+                for r in range(1, freq):
+                    b = (a + r) % freq
+                    sends.at[r - 1][...] = part[:, b * w:(b + 1) * w].astype(BF16)
+
+    def level(z, _):
+        owner = z // L
+        zl = z - owner * L
+        back = lax.rem(d - owner + depth, depth)
+
+        @pl.when(back == 0)
+        def _():
+            s_now[...] = slow[zl]
+
+        if got:
+            r = jnp.maximum(back - 1, 0)
+
+            @pl.when(jnp.logical_and(back > 0, zl == 0))
+            def _():
+                s_now[...] = got[0][r].astype(F32) + 1.0
+
+        if len(got) > 1:
+            @pl.when(jnp.logical_and(back > 0, zl > 0))
+            def _():
+                s_now[...] = got[1][r, jnp.maximum(zl - 1, 0)].astype(F32) + 1.0
+
+        for count in plan.counts(step):
+            def go():
+                if count == 0:
+                    part[...] = jnp.zeros((n, n), F32)
+                else:
+                    oms = [om[0, f0 + j] for j in range(count)]
+                    level_math(n, oms, s_now, T, K2, win, st, part, P, c, D)
+            if len(plan.counts(step)) == 1:
+                go()
+            else:
+                pl.when(nf == count)(go)
+
+        @pl.when(back == 0)
+        def _():
+            split(keep_own.at[zl], send_own.at[:, zl])
+
+        if keep_oth is not None:
+            @pl.when(back > 0)
+            def _():
+                to = jnp.maximum(depth - back - 1, 0)
+                split(keep_oth.at[to, zl], send_oth.at[:, to, zl])
+
+        return 0
+
+    lo, hi = plan.span(step, d)
+    lax.fori_loop(lo, hi, level, 0)
+
+
+def enter(plan, om_h, slow_h, T_h, K2_h, win_h, src, rcv, om_out, slow, T, K2, win, st, keep_own, send_own, keep_oth,
+          send_oth, om, raw, *rest):
+    n, fronts = plan.n, plan.fronts
+    sem_in, sem_t = rest[-2:]
+    d, nf, f0 = plan.share()
 
     def moves(j):
         fr = jnp.minimum(f0 + j, fronts - 1)
@@ -229,7 +320,7 @@
     ]
 
     def each(j, act):
-        if j < fronts // depth:
+        if j < plan.base:
             act()
         else:
             pl.when(j < nf)(act)
@@ -246,79 +337,26 @@
     each(0, lambda: begin(0))
     for m in small:
         m.start()
-    for j in range(1, slots):
+    for j in range(1, plan.slots):
         each(j, functools.partial(begin, j))
-    for j in range(slots):
+    for j in range(plan.slots):
         each(j, functools.partial(ready, j))
     for m in small:
         m.wait()
     for f in range(fronts):
         om_out[0, f] = om[0, f]
-
-    def level(z, _):
-        level_math(n, [om[0, f0 + j] for j in range(slots)], slow.at[z], T, K2, win, st, own_out.at[z], P, c, D)
-        return 0
-
-    lax.fori_loop(0, jnp.where(d == 0, L, 0), level, 0)
-
-
-def other_levels(dims, om, st_in, slow, got, own_in, T, K2, win, keep_own, send_own, keep_oth, send_oth, st,
-                 s_now, part, P, c, D):
-    n, slots, L, fronts, depth, freq = dims
-    d, nf, f0 = share(fronts, depth)
-    fq = lax.axis_index("freq")
-    lo = jnp.where(d == 0, L, 0)
-    w = n // freq
-
-    def split(ref, keep, sends):
-        for a in range(freq):
-            @pl.when(fq == a)
-            def _():
-                keep[...] = ref[:, a * w:(a + 1) * w]
-                for r in range(1, freq):
-                    b = (a + r) % freq
-                    sends.at[r - 1][...] = ref[:, b * w:(b + 1) * w].astype(BF16)
-
-    @pl.when(lo > 0)
-    def _():
-        for z in range(L):
-            split(own_in.at[z], keep_own.at[z], send_own.at[:, z])
-
-    def level(z, _):
-        owner = z // L
-        zl = z - owner * L
-        back = lax.rem(d - owner + depth, depth)
-
-        @pl.when(back == 0)
-        def _():
-            s_now[...] = slow[zl]
-
-        @pl.when(back > 0)
-        def _():
-            s_now[...] = got[jnp.maximum(back - 1, 0), zl].astype(F32) + 1.0
-
-        for count in sorted({slots, fronts // depth} - {0}):
-            @pl.when(nf == count)
-            def _():
-                level_math(n, [om[0, f0 + j] for j in range(count)], s_now, T, K2, win, st, part, P, c, D)
-
-        if fronts < depth:
-            @pl.when(nf == 0)
-            def _():
-                part[...] = jnp.zeros((n, n), F32)
-
-        @pl.when(back == 0)
-        def _():
-            split(part, keep_own.at[zl], send_own.at[:, zl])
-
-        @pl.when(back > 0)
-        def _():
-            r = jnp.maximum(depth - back - 1, 0)
-            split(part, keep_oth.at[r, zl], send_oth.at[:, r, zl])
-
-        return 0
-
-    lax.fori_loop(lo, depth * L, level, 0)
+    run_levels(plan, 0, om, slow, (), T, K2, win, st, keep_own, send_own, keep_oth, send_oth, *rest[:-2])
+
+
+def carry_on(plan, step, n_got, n_out, n_after, *refs):
+    om, slow, T, K2, win = refs[:5]
+    got = refs[5:5 + n_got]
+    here = 5 + n_got + n_out + n_after
+    outs = refs[here:here + n_out]
+    work = refs[here + n_out:]
+    if n_out == 3:
+        outs = (*outs, None, None)
+    run_levels(plan, step, om, slow, got, T, K2, win, *outs, *work)
 
 
 def place(dims, start, own, got, out, padded):
@@ -364,52 +402,65 @@
     h = n // 2
     fronts, L = source.shape[1], slowness.shape[1]
     depth, freq, shots = lax.axis_size("depth"), lax.axis_size("freq"), lax.axis_size("shot")
+    plan = Plan(n, L, fronts, depth, freq)
     T, K2, win = make_tables(n)
-    slots = -(-fronts // depth)
-    w = n // freq
-    S = jax.ShapeDtypeStruct
-    V = pltpu.VMEM
+    slots, w = plan.slots, n // freq
+    S, V = jax.ShapeDtypeStruct, pltpu.VMEM
     slow = slowness[0]
 
-    sent = (slow - 1.0).astype(BF16)
-    got = jnp.stack([shift(sent, "depth", r) for r in range(1, depth)])
-
-    math_scratch = [V((slots, 2, h + 8, n), F32), V((slots, 2, n, n), F32), V((3, n, n), F32)]
-    state, own_a, slow_v, T_v, K2_v, win_v, om = pl.pallas_call(
-        functools.partial(first_levels, (n, slots, L, fronts, depth)),
-        out_shape=(S((slots, 2, 2, n, n), BF16), S((L, n, n), F32), S((L, n, n), F32), S((4, 2, n, n), BF16),
-                   S((h + 8, h), F32), S((n, n), F32), S((1, fronts), F32)),
+    def known(part):
+        sent = (part - 1.0).astype(BF16)
+        return jnp.stack([shift(sent, "depth", r) for r in range(1, depth)])
+
+    got = [known(slow[0])]
+    if L > 1:
+        got.append(known(slow[1:]))
+
+    work = [V((n, n), F32), V((n, n), F32), V((slots, 2, h + 8, n), F32), V((slots, 2, n, n), F32), V((3, n, n), F32)]
+    share_own = [S((L, n, w), F32), S((freq - 1, L, n, w), BF16)]
+    share_oth = [S((depth - 1, L, n, w), F32), S((freq - 1, depth - 1, L, n, w), BF16)]
+    cost = pl.CostEstimate(flops=4 * 10**9, bytes_accessed=10**7, transcendentals=10**6)
+    tables = [S((1, fronts), F32), S((L, n, n), F32), S((4, 2, n, n), BF16), S((h + 8, h), F32), S((n, n), F32)]
+    state = [S((slots, 2, 2, n, n), BF16), *share_own, *share_oth]
+    done = pl.pallas_call(
+        functools.partial(enter, plan),
+        out_shape=(*tables, *state),
         in_specs=[HBM] * 7,
-        out_specs=(VM, VM, VM, VM, VM, VM, SM),
-        scratch_shapes=[pltpu.SMEM((1, fronts), F32), V((slots, 2, 2, n, n), F32)] + math_scratch
-        + [pltpu.SemaphoreType.DMA((slots, 2)), pltpu.SemaphoreType.DMA((5,))],
+        out_specs=(SM, *[VM] * 9),
+        scratch_shapes=[pltpu.SMEM((1, fronts), F32), V((slots, 2, 2, n, n), F32), *work,
+                        pltpu.SemaphoreType.DMA((slots, 2)), pltpu.SemaphoreType.DMA((5,))],
         compiler_params=params(40),
-        cost_estimate=pl.CostEstimate(flops=8 * 10**9, bytes_accessed=10**7, transcendentals=10**6),
-        name="first_levels",
+        cost_estimate=cost,
+        name="enter",
     )(*map(pinned, (omegas, slow, jnp.asarray(T), jnp.asarray(K2), jnp.asarray(win), source[0], receiver[0])))
-
-    keep_own, send_own, keep_oth, send_oth, _ = pl.pallas_call(
-        functools.partial(other_levels, (n, slots, L, fronts, depth, freq)),
-        out_shape=(S((L, n, w), F32), S((freq - 1, L, n, w), BF16),
-                   S((depth - 1, L, n, w), F32), S((freq - 1, depth - 1, L, n, w), BF16),
-                   S(state.shape, state.dtype)),
-        in_specs=[SM, VM, VM, VM, VM, VM, VM, VM],
-        out_specs=(VM, VM, VM, VM, VM),
-        input_output_aliases={1: 4},
-        scratch_shapes=[V((n, n), F32), V((n, n), F32)] + math_scratch,
-        compiler_params=params(32),
-        cost_estimate=pl.CostEstimate(flops=8 * 10**9, bytes_accessed=10**7, transcendentals=10**6),
-        name="other_levels",
-    )(om, state, slow_v, got, own_a, T_v, K2_v, win_v)
-
-    own, oth = keep_own, keep_oth
+    fixed, moving = done[:5], done[5:]
+
+    def carry(step, got, moving, after=()):
+        m = len(moving)
+        return pl.pallas_call(
+            functools.partial(carry_on, plan, step, len(got), m, len(after)),
+            out_shape=tuple(S(a.shape, a.dtype) for a in moving),
+            in_specs=[SM, *[VM] * (4 + len(got) + m + len(after))],
+            out_specs=(VM,) * m,
+            input_output_aliases={5 + len(got) + i: i for i in range(m)},
+            scratch_shapes=work,
+            compiler_params=params(40),
+            cost_estimate=cost,
+            name="levels_" + str(step),
+        )(*fixed, *got, *moving, *after)
+
+    moving = carry(1, got[:1], moving)
+    *moving, keep_oth, send_oth = carry(2, got, moving)
+    oth = keep_oth
     for r in range(1, freq):
         oth = oth + shift(send_oth[r - 1], "freq", r).astype(F32)
+    oth = oth.astype(BF16)
+    moving = carry(3, (), moving)
+    arrived = jnp.stack([shift(oth[r - 1], "depth", r) for r in range(1, depth)])
+    _, own, send_own = carry(4, (), moving, after=[oth])
     for r in range(1, freq):
         own = own + shift(send_own[r - 1], "freq", r).astype(F32)
-    oth = oth.astype(BF16)
-    own, start = lax.optimization_barrier((own, shot_start))
-    arrived = jnp.stack([shift(oth[r - 1], "depth", r) for r in range(1, depth)])
+    start = jnp.maximum(shot_start, 0)
 
     blocks = pl.pallas_call(
         functools.partial(place, (n, L, shots, depth - 1)),

time: 33.4 us -> 37.4 us (1.12)
  starting transfers between devices: 10.7 us -> 16.6 us
  Pallas kernels: 13.1 us -> 10.9 us
    ppermute x7 -> x8, starting transfers between devices: 10.7 us -> 16.6 us  [shift(): lax.ppermute(array, axis, [(i, (i + by) % size) for i in range(size)])]
    pallas_call x2 -> x5, Pallas kernels: 12.2 us -> 10.1 us  [the longest x4 5.04 us: carry(): pl.pallas_call(functools.partial(carry_on, plan, step, len(got), m, len(a...]
    ppermute x7 -> x8, waiting for transfers between devices: 7.58 us -> 7.76 us  [shift(): lax.ppermute(array, axis, [(i, (i + by) % size) for i in range(size)])]
    convert_element_type x1 -> x2, other arithmetic: 1.08 us -> 1.1 us  [the longest x1 1.07 us: known(): sent = (part - 1.0).astype(BF16)]
  transfers between devices with their start and end apart: 7 -> 8, of which waited for: 5 -> 4; matrix products, arithmetic and copies ran while one was open for 0% -> 0% of each run, Pallas kernels for 22% -> 20%
where the time goes in v5:
time: 37.4 us; the launch traced here: 37.2 us
  starting transfers between devices  16.6 us (44%)
  Pallas kernels  10.9 us (29%)
  waiting for transfers between devices  7.76 us (21%)
  other arithmetic  1.12 us (3%)
  between operations  0.75 us (2%)
    ppermute x8, starting transfers between devices, shift(): lax.ppermute(array, axis, [(i, (i + by) % size) for i in range(size)])  16.6 us
    ppermute x8, waiting for transfers between devices, shift(): lax.ppermute(array, axis, [(i, (i + by) % size) for i in range(size)])  7.76 us
    pallas_call x4, Pallas kernels, carry(): pl.pallas_call(functools.partial(carry_on, plan, step, len(got), m, len(a...  5.04 us
    pallas_call x1, Pallas kernels, local(): pl.pallas_call(functools.partial(enter, plan), out_shape=(*tables, *state...  5.01 us
    convert_element_type x1, other arithmetic, known(): sent = (part - 1.0).astype(BF16)  1.07 us
  transfers between devices with their start and end apart: 8, of which 4 were waited for; matrix products, arithmetic and copies ran while one was open for 0% of the time, Pallas kernels for 20%

profile of v5, /device:TPU:0, one launch (start us, length us, event | category | flops | bytes accessed | tf_op | source)
XLA Modules:
  0.0 37.2 jit_solution(4794154585541684065)
XLA Ops:
  0.0 1.1 %fusion.1 = (bf16[1,256,256]{2,1,0:T(8,128)(2,1)S(1)}, bf16[256,256]{1,0:T(8,128)(2,1)S(1)}) fusion(f32[1,2,256,256]{3,2,1,0:T(8,128)} %param.10), kind=kLoop, calls=%fused_computation.5 | loop fusion | flops 262144 | bytes 786432 | tf_op jit(solution)/shard_map/convert_element_type | solution.py:412
  1.1 3.0 %collective-permute-start = (bf16[256,256]{1,0:T(8,128)(2,1)S(1)}, bf16[256,256]{1,0:T(8,128)(2,1)S(1)}, u32[]{:S(2)}, u32[]{:S(2)}) collective-permute-start(bf16[256,256]{1,0:T(8,128)(2,1)S(1)} %get-tuple-element.56), channel_id=1, source_target_pairs={{0,2},{2,0},{1,3},{3,1},{4,6},{6,4},{5,7},{7,5},{8,10},{10,8},{9,1... | collective-permute-start | bytes 393224 | tf_op jit(solution)/shard_map/ppermute | solution.py:397
  4.1 0.1 collective-permute-start.1
  4.2 5.0 %enter.1 = (f32[1,3]{1,0:T(1,128)S(1)}, f32[2,256,256]{2,1,0:T(8,128)S(1)}, bf16[4,2,256,256]{3,2,1,0:T(8,128)(2,1)S(1)}, f32[136,128]{1,0:T(8,128)S(1)}, f32[25...) custom-call(f32[1,3]{1,0:T(1,128)} %om_h.1, ...), custom_call_target="tpu_custom_call" | custom-call | flops 4000000000 | bytes 10000000 | tf_op jit(solution)/shard_map/enter/pallas_call | solution.py:425
  9.2 0.0 collective-permute-done
  9.2 1.9 %levels_1.1 = (bf16[2,2,2,256,256]{4,3,2,1,0:T(8,128)(2,1)S(1)}, f32[2,256,128]{2,1,0:T(8,128)S(1)}, bf16[1,2,256,128]{3,2,1,0:T(8,128)(2,1)S(1)}, f32[1,2,256,1...) custom-call(f32[1,3]{1,0:T(1,128)S(1)} %get-tuple-element.30.refs_0_, ...), custom_call_target="tpu_custom_call", output_to_operand_aliasing={{0}: (6, {}), {1}: (7, {}), {2}: (8, {}), {3}: (9, {}), {4}... | custom-call | flops 4000000000 | bytes 10000000 | tf_op jit(solution)/shard_map/levels_1/pallas_call | solution.py:440
  11.1 0.0 collective-permute-done.1
  11.1 1.9 %levels_2.1 = (bf16[2,2,2,256,256]{4,3,2,1,0:T(8,128)(2,1)S(1)}, f32[2,256,128]{2,1,0:T(8,128)S(1)}, bf16[1,2,256,128]{3,2,1,0:T(8,128)(2,1)S(1)}, f32[1,2,256,1...) custom-call(f32[1,3]{1,0:T(1,128)S(1)} %get-tuple-element.30.refs_0_, ...), custom_call_target="tpu_custom_call", output_to_operand_aliasing={{0}: (7, {}), {1}: (8, {}), {2}: (9, {}), {3}: (10, {}), {4... | custom-call | flops 4000000000 | bytes 10000000 | tf_op jit(solution)/shard_map/levels_2/pallas_call | solution.py:440
  13.0 0.1 collective-permute-start.2
  13.1 0.6 %levels_3.1 = (bf16[2,2,2,256,256]{4,3,2,1,0:T(8,128)(2,1)S(1)}, f32[2,256,128]{2,1,0:T(8,128)S(1)}, bf16[1,2,256,128]{3,2,1,0:T(8,128)(2,1)S(1)}) custom-call(f32[1,3]{1,0:T(1,128)S(1)} %get-tuple-element.30.refs_0_, f32[2,256,256]{2,1,0:T(8,128)S(1)} %get-tuple-element.31.refs_1_, ...), custom_call_target="tpu_custom_call", output_to_operand_aliasing={{0}: (5, {}), {1}: (6, {}), {2}: (7, {})} | custom-call | flops 4000000000 | bytes 10000000 | tf_op jit(solution)/shard_map/levels_3/pallas_call | solution.py:440
  13.6 0.8 %collective-permute-done.2 = bf16[1,2,256,128]{3,2,1,0:T(8,128)(2,1)S(1)} collective-permute-done((bf16[1,2,256,128]{3,2,1,0:T(8,128)(2,1)S(1)}, bf16[1,2,256,128]{3,2,1,0:T(8,128)(2,1)S(1)}, u32[]{:S(2)}, u32[]{:S(2)}) %collective-permute-start.2) | collective-permute-done | bytes 131104 | tf_op jit(solution)/shard_map/ppermute | solution.py:397
  14.4 0.7 %levels_4.1 = (bf16[2,2,2,256,256]{4,3,2,1,0:T(8,128)(2,1)S(1)}, f32[2,256,128]{2,1,0:T(8,128)S(1)}, bf16[1,2,256,128]{3,2,1,0:T(8,128)(2,1)S(1)}) custom-call(f32[1,3]{1,0:T(1,128)S(1)} %get-tuple-element.30.refs_0_, f32[2,256,256]{2,1,0:T(8,128)S(1)} %get-tuple-element.31.refs_1_, ...), custom_call_target="tpu_custom_call", output_to_operand_aliasing={{0}: (5, {}), {1}: (6, {}), {2}: (7, {})} | custom-call | flops 4000000000 | bytes 10000000 | tf_op jit(solution)/shard_map/levels_4/pallas_call | solution.py:440
  15.2 0.2 collective-permute-start.3
  16.0 7.7 %collective-permute-start.4 = (bf16[2,256,128]{2,1,0:T(8,128)(2,1)S(1)}, bf16[2,256,128]{2,1,0:T(8,128)(2,1)S(1)}, u32[]{:S(2)}, u32[]{:S(2)}) collective-permute-start(bf16[2,256,128]{2,1,0:T(8,128)(2,1)S(1)} %bitcast.21), channel_id=1, source_target_pairs={{0,2},{2,0},{1,3},{3,1},{4,6},{6,4},{5,7},{7,5},{8,10},{10,8},{9,1... | collective-permute-start | bytes 393224 | tf_op jit(solution)/shard_map/ppermute | solution.py:397
  23.7 0.0 collective-permute-done.3
  23.8 3.7 %collective-permute-done.4 = bf16[2,256,128]{2,1,0:T(8,128)(2,1)S(1)} collective-permute-done((bf16[2,256,128]{2,1,0:T(8,128)(2,1)S(1)}, bf16[2,256,128]{2,1,0:T(8,128)(2,1)S(1)}, u32[]{:S(2)}, u32[]{:S(2)}) %collective-permute-start.4) | collective-permute-done | bytes 131104 | tf_op jit(solution)/shard_map/ppermute | solution.py:397
  27.4 0.1 place.1
  27.6 1.6 %collective-permute-start.5 = (bf16[2,128,128]{2,1,0:T(8,128)(2,1)S(1)}, bf16[2,128,128]{2,1,0:T(8,128)(2,1)S(1)}, u32[]{:S(2)}, u32[]{:S(2)}) collective-permute-start(bf16[2,128,128]{2,1,0:T(8,128)(2,1)S(1)} %get-tuple-element.59), channel_id=1, source_target_pairs={{0,4},{4,8},{8,12},{12,0},{1,5},{5,9},{9,13},{13,1},{2,6},{6,10},{... | collective-permute-start | bytes 196616 | tf_op jit(solution)/shard_map/ppermute | solution.py:397
  29.2 2.6 %collective-permute-start.6 = (bf16[2,128,128]{2,1,0:T(8,128)(2,1)S(1)}, bf16[2,128,128]{2,1,0:T(8,128)(2,1)S(1)}, u32[]{:S(2)}, u32[]{:S(2)}) collective-permute-start(bf16[2,128,128]{2,1,0:T(8,128)(2,1)S(1)} %get-tuple-element.58), channel_id=1, source_target_pairs={{0,8},{4,12},{8,0},{12,4},{1,9},{5,13},{9,1},{13,5},{2,10},{6,14},... | collective-permute-start | bytes 196616 | tf_op jit(solution)/shard_map/ppermute | solution.py:397
  31.8 1.3 %collective-permute-start.7 = (bf16[2,128,128]{2,1,0:T(8,128)(2,1)S(1)}, bf16[2,128,128]{2,1,0:T(8,128)(2,1)S(1)}, u32[]{:S(2)}, u32[]{:S(2)}) collective-permute-start(bf16[2,128,128]{2,1,0:T(8,128)(2,1)S(1)} %get-tuple-element.57), channel_id=1, source_target_pairs={{0,12},{4,0},{8,4},{12,8},{1,13},{5,1},{9,5},{13,9},{2,14},{6,2},{... | collective-permute-start | bytes 196616 | tf_op jit(solution)/shard_map/ppermute | solution.py:397
  33.1 1.4 %collective-permute-done.5.refs_1_ = bf16[2,128,128]{2,1,0:T(8,128)(2,1)S(1)} collective-permute-done((bf16[2,128,128]{2,1,0:T(8,128)(2,1)S(1)}, bf16[2,128,128]{2,1,0:T(8,128)(2,1)S(1)}, u32[]{:S(2)}, u32[]{:S(2)}) %collective-permute-start.5) | collective-permute-done | bytes 65568 | tf_op jit(solution)/shard_map/ppermute | solution.py:397
  34.5 2.0 %collective-permute-done.6.refs_2_ = bf16[2,128,128]{2,1,0:T(8,128)(2,1)S(1)} collective-permute-done((bf16[2,128,128]{2,1,0:T(8,128)(2,1)S(1)}, bf16[2,128,128]{2,1,0:T(8,128)(2,1)S(1)}, u32[]{:S(2)}, u32[]{:S(2)}) %collective-permute-start.6) | collective-permute-done | bytes 65568 | tf_op jit(solution)/shard_map/ppermute | solution.py:397
  36.5 0.0 collective-permute-done.7.refs_3_
  36.5 0.7 %gather.1 = f32[128,2,128]{2,1,0:T(2,128)} custom-call(bf16[2,128,128]{2,1,0:T(8,128)(2,1)S(1)} %get-tuple-element.60.refs_0_, bf16[2,128,128]{2,1,0:T(8,128)(2,1)S(1)} %collective-permute-done.5.refs_1_, bf16[2,128,128]{2,1,0:T(8,128)(2,1)S(1)} %collective-permute-done.6.refs_2_, bf16[2,128,128]{2,1,0:T(8,128)(2,1)S(1)} %collective-permute-done.7.refs_3_), custom_call_target="tpu_custom_call" | custom-call | tf_op jit(solution)/shard_map/gather/pallas_call | solution.py:475
  (3 shorter events, 0.1 us)
Async XLA Ops:
  1.1 8.1 %collective-permute-start = (bf16[256,256]{1,0:T(8,128)(2,1)S(1)}, bf16[256,256]{1,0:T(8,128)(2,1)S(1)}, u32[]{:S(2)}, u32[]{:S(2)}) collective-permute-start(bf16[256,256]{1,0:T(8,128)(2,1)S(1)} %get-tuple-element.56), channel_id=1, source_target_pairs={{0,2},{2,0},{1,3},{3,1},{4,6},{6,4},{5,7},{7,5},{8,10},{10,8},{9,1... | collective-permute-start | bytes 393224 | tf_op jit(solution)/shard_map/ppermute | solution.py:397
  4.1 7.0 %collective-permute-start.1 = (bf16[1,256,256]{2,1,0:T(8,128)(2,1)S(1)}, bf16[1,256,256]{2,1,0:T(8,128)(2,1)S(1)}, u32[]{:S(2)}, u32[]{:S(2)}) collective-permute-start(bf16[1,256,256]{2,1,0:T(8,128)(2,1)S(1)} %get-tuple-element.55), channel_id=1, source_target_pairs={{0,2},{2,0},{1,3},{3,1},{4,6},{6,4},{5,7},{7,5},{8,10},{10,8},{9,1... | collective-permute-start | bytes 393224 | tf_op jit(solution)/shard_map/ppermute | solution.py:397
  13.0 1.4 %collective-permute-start.2 = (bf16[1,2,256,128]{3,2,1,0:T(8,128)(2,1)S(1)}, bf16[1,2,256,128]{3,2,1,0:T(8,128)(2,1)S(1)}, u32[]{:S(2)}, u32[]{:S(2)}) collective-permute-start(bf16[1,2,256,128]{3,2,1,0:T(8,128)(2,1)S(1)} %bitcast.27), channel_id=1, source_target_pairs={{0,1},{1,0},{2,3},{3,2},{4,5},{5,4},{6,7},{7,6},{8,9},{9,8},{10,11... | collective-permute-start | bytes 393224 | tf_op jit(solution)/shard_map/ppermute | solution.py:397
  15.2 8.6 %collective-permute-start.3 = (bf16[2,256,128]{2,1,0:T(8,128)(2,1)S(1)}, bf16[2,256,128]{2,1,0:T(8,128)(2,1)S(1)}, u32[]{:S(2)}, u32[]{:S(2)}) collective-permute-start(bf16[2,256,128]{2,1,0:T(8,128)(2,1)S(1)} %bitcast.26), channel_id=1, source_target_pairs={{0,1},{1,0},{2,3},{3,2},{4,5},{5,4},{6,7},{7,6},{8,9},{9,8},{10,11... | collective-permute-start | bytes 393224 | tf_op jit(solution)/shard_map/ppermute | solution.py:397
  16.0 11.4 %collective-permute-start.4 = (bf16[2,256,128]{2,1,0:T(8,128)(2,1)S(1)}, bf16[2,256,128]{2,1,0:T(8,128)(2,1)S(1)}, u32[]{:S(2)}, u32[]{:S(2)}) collective-permute-start(bf16[2,256,128]{2,1,0:T(8,128)(2,1)S(1)} %bitcast.21), channel_id=1, source_target_pairs={{0,2},{2,0},{1,3},{3,1},{4,6},{6,4},{5,7},{7,5},{8,10},{10,8},{9,1... | collective-permute-start | bytes 393224 | tf_op jit(solution)/shard_map/ppermute | solution.py:397
  27.6 6.9 %collective-permute-start.5 = (bf16[2,128,128]{2,1,0:T(8,128)(2,1)S(1)}, bf16[2,128,128]{2,1,0:T(8,128)(2,1)S(1)}, u32[]{:S(2)}, u32[]{:S(2)}) collective-permute-start(bf16[2,128,128]{2,1,0:T(8,128)(2,1)S(1)} %get-tuple-element.59), channel_id=1, source_target_pairs={{0,4},{4,8},{8,12},{12,0},{1,5},{5,9},{9,13},{13,1},{2,6},{6,10},{... | collective-permute-start | bytes 196616 | tf_op jit(solution)/shard_map/ppermute | solution.py:397
  29.2 7.3 %collective-permute-start.6 = (bf16[2,128,128]{2,1,0:T(8,128)(2,1)S(1)}, bf16[2,128,128]{2,1,0:T(8,128)(2,1)S(1)}, u32[]{:S(2)}, u32[]{:S(2)}) collective-permute-start(bf16[2,128,128]{2,1,0:T(8,128)(2,1)S(1)} %get-tuple-element.58), channel_id=1, source_target_pairs={{0,8},{4,12},{8,0},{12,4},{1,9},{5,13},{9,1},{13,5},{2,10},{6,14},... | collective-permute-start | bytes 196616 | tf_op jit(solution)/shard_map/ppermute | solution.py:397
  31.8 4.7 %collective-permute-start.7 = (bf16[2,128,128]{2,1,0:T(8,128)(2,1)S(1)}, bf16[2,128,128]{2,1,0:T(8,128)(2,1)S(1)}, u32[]{:S(2)}, u32[]{:S(2)}) collective-permute-start(bf16[2,128,128]{2,1,0:T(8,128)(2,1)S(1)} %get-tuple-element.57), channel_id=1, source_target_pairs={{0,12},{4,0},{8,4},{12,8},{1,13},{5,1},{9,5},{13,9},{2,14},{6,2},{... | collective-permute-start | bytes 196616 | tf_op jit(solution)/shard_map/ppermute | solution.py:397
